TPU v7x, 128 devices: a whole 4x4x4 slice. The times are simulated.
128 devices in a mesh: dp: 8 (over z_hi, y), fsdp: 16 (over x, z_lo, core).
Axes of the slice: x: 4, y: 4, z: 4 (z_hi: 2, z_lo: 2; z = z_hi * 2 + z_lo), core: 2. Of those that a mesh axis runs over, the one named last changes fastest.
Arguments:
- tokens: bfloat16 [65536, 8192], P(('dp', 'fsdp')), may hold values from -6 to 6
- cotangent: bfloat16 [65536, 1024], P(('dp', 'fsdp')), may hold values from -6 to 6
- weight: bfloat16 [8192, 1024], P('fsdp'), may hold values from -0.0625 to 0.0625
- feedback: float32 [8, 8192, 1024], P('dp', 'fsdp'), may hold values from -24 to 24
- q_factor: float32 [1024, 64], replicated, may hold values from -6 to 6
Outputs:
- input_grad: bfloat16 [65536, 8192], P(('dp', 'fsdp'))
- q_next: float32 [1024, 64], replicated
- feedback_next: float32 [8, 8192, 1024], P('dp', 'fsdp')
All inputs are finite; a program needn't handle non-finite values.
Results may differ from a plain program's by a relative error of at most 0.012.
Values may be sent and summed in bfloat16 or wider, within the bound.
A program may use at most 128 MiB of HBM per device.

v0:
```python
import math

import jax
import jax.numpy as jnp
from jax import lax
from jax.sharding import PartitionSpec as P

highest = lax.Precision.HIGHEST


def exact_dot(left, right):
    return jnp.dot(left, right, precision=highest, preferred_element_type=jnp.float32)


def lower_solve(lower_factor, right_side):
    return lax.linalg.triangular_solve(lower_factor, right_side, left_side=True, lower=True)


def per_device(tokens, cotangent, weight, feedback, q_factor):
    groups = lax.axis_size("dp")
    members = lax.axis_size("fsdp")
    tok_dev = tokens.shape[0]
    grad_scale = 1.0 / math.sqrt(tok_dev * members)
    product = lax.dot_general(
        cotangent,
        lax.all_gather(weight, "fsdp", axis=0, tiled=True),
        (((1,), (1,)), ((), ())),
        preferred_element_type=jnp.float32,
    )
    input_grad = product.astype(jnp.bfloat16)
    grad_rows = (
        lax.psum_scatter(
            lax.dot_general(
                tokens, cotangent, (((0,), (0,)), ((), ())), preferred_element_type=jnp.float32
            ).astype(jnp.bfloat16),
            "fsdp",
            scatter_dimension=0,
            tiled=True,
        ).astype(jnp.float32)
        * grad_scale
    )
    merged = feedback[0] + grad_rows
    p_local = exact_dot(merged, q_factor)
    p_sum = lax.psum(p_local.astype(jnp.bfloat16), "dp").astype(jnp.float32) / groups
    gram_part = exact_dot(p_sum.T, p_sum)
    gram_sum = lax.psum(gram_part, "fsdp")
    lower_factor = jnp.linalg.cholesky(gram_sum)
    p_hat = lower_solve(lower_factor, p_sum.T).T
    q_next = lax.psum(exact_dot(merged.T, p_hat), ("dp", "fsdp")) / groups
    feedback_next = merged - exact_dot(p_hat, q_next.T)
    return (input_grad, q_next, feedback_next[None])


def solution(mesh):
    placed = (
        P(("dp", "fsdp"), None),
        P(("dp", "fsdp"), None),
        P("fsdp", None),
        P("dp", "fsdp", None),
        P(),
    )
    return jax.shard_map(
        per_device,
        mesh=mesh,
        in_specs=placed,
        out_specs=(P(("dp", "fsdp"), None), P(), P("dp", "fsdp", None)),
        check_vma=False,
    )
```

profile of v0, /device:TPU:0, one launch (start us, length us, event | category | flops | bytes accessed | tf_op | source)
XLA Modules:
  0.0 550.0 jit_solution(7272778245979105122)
XLA Ops:
  7.2 0.0 copy-start
  7.2 0.0 reduce-scatter.2.cloned.1.call-start
  7.2 1.2 copy-done
  8.4 15.9 %convolution_convert_fusion = bf16[8192,1024]{1,0:T(8,128)(2,1)} fusion(bf16[512,8192]{1,0:T(8,128)(2,1)} %param.5, bf16[512,1024]{1,0:T(8,128)(2,1)S(1)} %copy-done), kind=kOutput, calls=%fused_computation | convolution fusion | flops 8598323200 | bytes 26214400 | tf_op jit(solution)/shard_map/dot_general | solution.py:33
  24.3 0.0 reduce-scatter.2.cloned.1.call-update
  24.3 0.0 all-reduce.3.cloned.1.call-start
  24.4 178.4 %reduce-scatter.2.cloned.1.call-done = bf16[512,1024]{1,0:T(8,128)(2,1)} async-done(((bf16[8192,1024]{1,0:T(8,128)(2,1)}), bf16[512,1024]{1,0:T(8,128)(2,1)}) %reduce-scatter.2.cloned.1.call-update) | async-done | bytes 1048592 | tf_op jit(solution)/shard_map/reduce_scatter | solution.py:32
  202.7 0.0 copy-done.1
  202.7 0.0 copy-done.3
  202.8 4.2 convolution_convert_fusion.2
  206.9 0.0 all-reduce.3.cloned.1.call-update
  206.9 0.0 all-gather.2.cloned.1.call-start
  207.0 0.7 all-gather.2.cloned.1.call-update
  207.7 0.0 all-reduce.5.cloned.1.call-start
  207.7 89.1 %all-reduce.3.cloned.1.call-done = bf16[512,64]{0,1:T(8,128)(2,1)} async-done(((bf16[512,64]{0,1:T(8,128)(2,1)}), bf16[512,64]{0,1:T(8,128)(2,1)}) %all-reduce.3.cloned.1.call-update) | async-done | bytes 65552 | tf_op jit(solution)/shard_map/psum | solution.py:44
  296.8 1.2 fusion.2
  298.0 54.5 %psum.22 = f32[64,64]{0,1:T(8,128)S(1)} all-reduce(f32[64,64]{0,1:T(8,128)S(1)} %fusion.2), channel_id=1, replica_groups=mesh['dp'=8,'fsdp'=16] {'fsdp'}, use_global_device_ids=true, to_apply=%region_2.0 | all-reduce | flops 4096 | bytes 32768 | tf_op jit(solution)/shard_map/psum | solution.py:46
  352.5 0.1 copy.9
  352.6 5.8 %cholesky.16 = f32[64,64]{1,0:T(8,128)S(1)} custom-call(f32[64,64]{1,0:T(8,128)S(1)} %fusion.7), custom_call_target="Cholesky" | custom-call | tf_op jit(solution)/shard_map/jit(cholesky)/cholesky | solution.py:47
  358.5 0.6 compare_reduce_fusion
  359.1 0.7 fusion.5
  359.8 4.9 custom-call.6
  364.7 1.2 fusion.1
  365.9 3.6 fusion
  369.4 0.0 all-reduce.5.cloned.1.call-update
  369.5 19.6 %all-gather.2.cloned.1.call-done = bf16[8192,1024]{1,0:T(8,128)(2,1)} async-done(((bf16[512,1024]{1,0:T(8,128)(2,1)}), bf16[8192,1024]{1,0:T(8,128)(2,1)}) %all-gather.2.cloned.1.call-update) | async-done | bytes 16777232 | tf_op jit(solution)/shard_map/all_gather | solution.py:26
  389.0 29.6 %convolution_convert_fusion.1 = bf16[512,8192]{1,0:T(8,128)(2,1)} fusion(bf16[512,1024]{1,0:T(8,128)(2,1)S(1)} %copy-done, bf16[8192,1024]{1,0:T(8,128)(2,1)} %all-gather.2.cloned.1.call-done), kind=kOutput, calls=%fused_computation.1 | convolution fusion | flops 8594128896 | bytes 26214400 | tf_op jit(solution)/shard_map/dot_general | solution.py:24
  418.6 119.2 %all-reduce.5.cloned.1.call-done = f32[1024,64]{0,1:T(8,128)} async-done(((f32[1024,64]{0,1:T(8,128)}), f32[1024,64]{0,1:T(8,128)}) %all-reduce.5.cloned.1.call-update) | async-done | bytes 262160 | tf_op jit(solution)/shard_map/psum | solution.py:49
  537.9 1.0 broadcast_multiply_fusion
  538.8 0.0 copy-start.2
  538.9 4.6 subtract_bitcast_fusion
  543.5 0.0 copy-done.2
  (4 shorter events, 0.0 us)
Async XLA Ops:
  7.2 1.2 copy-start
  7.2 195.6 %reduce-scatter.2.cloned.1.call-start = ((), (), s32[]{:S(2)}) async-start(), calls=%async_computation.2 | async-start | bytes 17825792 | tf_op jit(solution)/shard_map/reduce_scatter | solution.py:32
  24.3 178.4 %copy-start.1 = (f32[1,512,1024]{2,1,0:T(8,128)S(1)}, f32[1,512,1024]{2,1,0:T(8,128)}, u32[]{:S(2)}) copy-start(f32[1,512,1024]{2,1,0:T(8,128)} %param.8) | copy-start | bytes 6291460
  24.3 178.4 %copy-start.3 = (f32[1024,64]{0,1:T(8,128)S(1)}, f32[1024,64]{0,1:T(8,128)}, u32[]{:S(2)}) copy-start(f32[1024,64]{0,1:T(8,128)} %param.9) | copy-start | bytes 786436
  24.3 272.5 %all-reduce.3.cloned.1.call-start = ((), (), s32[]{:S(2)}) async-start(), calls=%async_computation.3 | async-start | bytes 131072 | tf_op jit(solution)/shard_map/psum | solution.py:44
  206.9 182.1 %all-gather.2.cloned.1.call-start = ((), (), s32[]{:S(2)}) async-start(), calls=%async_computation.1 | async-start | bytes 17825792 | tf_op jit(solution)/shard_map/all_gather | solution.py:26
  207.7 330.2 %all-reduce.5.cloned.1.call-start = ((), (), s32[]{:S(2)}) async-start(), calls=%async_computation.4 | async-start | bytes 524288 | tf_op jit(solution)/shard_map/psum | solution.py:49
  538.8 4.7 copy-start.2
Sparse Core Ops, SparseCore 0:
  24.5 178.2 reduce-scatter.1
  207.1 89.7 all-reduce.2
  298.5 90.4 all-gather.1
  394.2 143.6 all-reduce.4
where the time goes:
time: 551 us; the launch traced here: 550 us
  waiting for transfers between devices  407 us (74%)
  matrix products  60.2 us (11%)
  blocking collectives  54.5 us (10%)
  between operations  13.8 us (3%)
  other arithmetic  13 us (2%)
    reduce_scatter x1, waiting for transfers between devices, per_device(): lax.psum_scatter(lax.dot_general(tokens, cotangent, (((0,), (0,)), ((), (...  178 us
    psum x1, waiting for transfers between devices, per_device(): q_next = lax.psum(exact_dot(merged.T, p_hat), ('dp', 'fsdp')) / groups  119 us
    psum x1, waiting for transfers between devices, per_device(): lax.psum(p_local.astype(jnp.bfloat16), 'dp').astype(jnp.float32) / groups  89.1 us
    psum x1, blocking collectives, per_device(): gram_sum = lax.psum(gram_part, 'fsdp')  54.5 us
    dot_general x1, matrix products, per_device(): lax.dot_general(cotangent, lax.all_gather(weight, 'fsdp', axis=0, tiled=T...  29.6 us
    all_gather x1, waiting for transfers between devices, per_device(): lax.all_gather(weight, 'fsdp', axis=0, tiled=True)  19.6 us
    dot_general x1, matrix products, per_device(): lax.dot_general(tokens, cotangent, (((0,), (0,)), ((), ())), preferred_el...  15.9 us
    dot_general x4, matrix products, exact_dot(): jnp.dot(left, right, precision=highest, preferred_element_type=jnp.float32)  13.6 us
  transfers between devices with their start and end apart: 4, of which 4 were waited for; matrix products, arithmetic and copies ran while one was open for 9% of the time, Pallas kernels for 0%

commit v1 on v0

v1 whole, which is shorter than its diff:
```python
import functools
import math

import jax
import jax.numpy as jnp
from jax import lax
from jax.experimental import pallas as pl
from jax.experimental.pallas import tpu as pltpu
from jax.sharding import PartitionSpec as P

MESH = pl.DeviceIdType.MESH
HIGHEST = lax.Precision.HIGHEST
F32 = jnp.float32
BF16 = jnp.bfloat16


def where_am_i():
    d = lax.axis_index("dp")
    f = lax.axis_index("fsdp")
    return d // 4, d % 4, f // 4, (f // 2) % 2, f % 2


def device(zh, y, x, zl, c):
    return (zh * 4 + y, x * 4 + zl * 2 + c)


def exact(left, right, dims):
    return lax.dot_general(left, right, (dims, ((), ())), precision=HIGHEST, preferred_element_type=F32)


def spread(src, slots, send_sem, recv_sem, me, targets):
    copies = []
    for k, target in enumerate(targets):
        copies.append(
            pltpu.make_async_remote_copy(
                src_ref=src(k),
                dst_ref=slots.at[me],
                send_sem=send_sem.at[k],
                recv_sem=recv_sem.at[k],
                device_id=target,
                device_id_type=MESH,
            )
        )
    for copy in copies:
        copy.start()
    return copies


def tail_kernel(
    grad_scale, feedback_ref, grad_ref, q_ref, qn_ref, fn_ref,
    merged, p_slots, g_slots, s_out, s1, s2, s3,
    p_send, p_recv, g_send, g_recv, s1_send, s1_recv, s2_send, s2_recv, s3_send, s3_recv,
):
    zh, y, x, zl, c = where_am_i()
    d = lax.axis_index("dp")
    f = lax.axis_index("fsdp")
    plane = x * 4 + y
    column = zh * 4 + zl * 2 + c

    group_of = [((d + k) % 8, f) for k in range(1, 8)]
    member_of = [(d, (f + k) % 16) for k in range(1, 16)]
    plane_at = [(plane + k) % 16 for k in range(1, 16)]
    plane_of = [device(zh, t % 4, t // 4, zl, c) for t in plane_at]
    column_at = [(column + k) % 8 for k in range(1, 8)]
    column_of = [device(t // 4, y, x, (t // 2) % 2, t % 2) for t in column_at]

    barrier = pltpu.get_barrier_semaphore()
    everyone = group_of + member_of + plane_of + column_of
    for target in everyone:
        pl.semaphore_signal(barrier, inc=1, device_id=target, device_id_type=MESH)

    merged[...] = feedback_ref[...] + grad_ref[...].astype(F32) * grad_scale
    p_slots[d] = exact(q_ref[...], merged[...], ((1,), (1,))).astype(BF16)
    pl.semaphore_wait(barrier, len(everyone))

    copies = spread(lambda k: p_slots.at[d], p_slots, p_send, p_recv, d, group_of)
    for copy in copies:
        copy.wait()
    total = p_slots[0].astype(F32)
    for k in range(1, 8):
        total = total + p_slots[k].astype(F32)
    factor = total * 0.125

    s_local = exact(factor, merged[...], ((1,), (0,))) * 0.125
    for i in range(4):
        for j in range(4):
            s_out[i * 4 + j] = s_local[16 * i : 16 * i + 16, 256 * j : 256 * j + 256]
    s1_copies = spread(lambda k: s_out.at[plane_at[k]], s1, s1_send, s1_recv, plane, plane_of)
    g_slots[f] = exact(factor, factor, ((1,), (1,)))
    g_copies = spread(lambda k: g_slots.at[f], g_slots, g_send, g_recv, f, member_of)
    s1[plane] = s_out[plane]
    for copy in s1_copies:
        copy.wait()
    part = s1[0]
    for k in range(1, 16):
        part = part + s1[k]
    s2[column] = part
    s2_copies = spread(lambda k: s2.at[column], s2, s2_send, s2_recv, column, column_of)

    for copy in g_copies:
        copy.wait()
    gram = g_slots[0]
    for k in range(1, 16):
        gram = gram + g_slots[k]
    row_id = lax.broadcasted_iota(jnp.int32, (64, 64), 0)
    lane_id = lax.broadcasted_iota(jnp.int32, (64, 64), 1)
    eye = jnp.where(row_id == lane_id, 1.0, 0.0).astype(F32)
    work = jnp.concatenate([eye, gram], axis=1)
    rows = lax.broadcasted_iota(jnp.int32, (64, 128), 0)

    def eliminate(work, k):
        pivot = jnp.broadcast_to(work[k : k + 1, 64 + k : 65 + k], (64, 128))
        column_k = jnp.broadcast_to(work[:, 64 + k : 65 + k], (64, 128))
        row_k = jnp.broadcast_to(work[k : k + 1, :], (64, 128))
        root = lax.rsqrt(pivot)
        root = root * (1.5 - 0.5 * pivot * root * root)
        scaled = row_k * root
        below = work - (column_k * root) * scaled
        return jnp.where(rows > k, below, jnp.where(rows == k, scaled, work))

    for k in range(16):
        work = eliminate(work, k)

    for copy in s2_copies:
        copy.wait()
    part = s2[0]
    for k in range(1, 8):
        part = part + s2[k]
    s3[plane] = part
    s3_copies = spread(lambda k: s3.at[plane], s3, s3_send, s3_recv, plane, plane_of)

    for k in range(16, 64):
        work = eliminate(work, k)
    inverse = work[:, :64]
    p_hat = jnp.transpose(exact(inverse, factor, ((1,), (0,))))

    for copy in s3_copies:
        copy.wait()
    s_total = jnp.concatenate(
        [jnp.concatenate([s3[i * 4 + j] for j in range(4)], axis=1) for i in range(4)], axis=0
    )
    q_next = exact(inverse, s_total, ((1,), (0,)))
    qn_ref[...] = q_next
    fn_ref[...] = merged[...] - exact(p_hat, q_next, ((1,), (0,)))


def tail(feedback, grad_rows, q_t, grad_scale):
    rows, width = feedback.shape
    rank = q_t.shape[0]
    vmem = pl.BlockSpec(memory_space=pltpu.VMEM)
    dma = pltpu.SemaphoreType.DMA
    return pl.pallas_call(
        functools.partial(tail_kernel, grad_scale),
        out_shape=(
            jax.ShapeDtypeStruct((rank, width), F32),
            jax.ShapeDtypeStruct((rows, width), F32),
        ),
        in_specs=[vmem] * 3,
        out_specs=(vmem, vmem),
        scratch_shapes=[
            pltpu.VMEM((rows, width), F32),
            pltpu.VMEM((8, rank, rows), BF16),
            pltpu.VMEM((16, rank, rank), F32),
            pltpu.VMEM((16, 16, 256), F32),
            pltpu.VMEM((16, 16, 256), F32),
            pltpu.VMEM((8, 16, 256), F32),
            pltpu.VMEM((16, 16, 256), F32),
            dma((7,)), dma((7,)), dma((15,)), dma((15,)), dma((15,)), dma((15,)),
            dma((7,)), dma((7,)), dma((15,)), dma((15,)),
        ],
        compiler_params=pltpu.CompilerParams(
            collective_id=1, has_side_effects=True, vmem_limit_bytes=48 * 1024 * 1024
        ),
        name="tail",
    )(feedback, grad_rows, q_t)


def per_device(tokens, cotangent, weight, feedback, q_factor):
    members = lax.axis_size("fsdp")
    grad_scale = 1.0 / math.sqrt(tokens.shape[0] * members)
    product = lax.dot_general(
        cotangent,
        lax.all_gather(weight, "fsdp", axis=0, tiled=True),
        (((1,), (1,)), ((), ())),
        preferred_element_type=F32,
    )
    input_grad = product.astype(BF16)
    grad_rows = lax.psum_scatter(
        lax.dot_general(
            tokens, cotangent, (((0,), (0,)), ((), ())), preferred_element_type=F32
        ).astype(BF16),
        "fsdp",
        scatter_dimension=0,
        tiled=True,
    )
    q_next, feedback_next = tail(feedback[0], grad_rows, q_factor.T, grad_scale)
    return (input_grad, q_next.T, feedback_next[None])


def solution(mesh):
    placed = (
        P(("dp", "fsdp"), None),
        P(("dp", "fsdp"), None),
        P("fsdp", None),
        P("dp", "fsdp", None),
        P(),
    )
    return jax.shard_map(
        per_device,
        mesh=mesh,
        in_specs=placed,
        out_specs=(P(("dp", "fsdp"), None), P(), P("dp", "fsdp", None)),
        check_vma=False,
    )
```

time: 551 us -> 343 us (0.62)
  waiting for transfers between devices: 407 us -> 229 us
  blocking collectives: 54.5 us -> 0 us
  Pallas kernels: 0 us -> 49.6 us
  matrix products: 60.2 us -> 45.5 us
  other arithmetic: 13 us -> 0 us
    psum x2 -> x0, waiting for transfers between devices: 208 us -> none  [the longest x1 119 us: per_device(): q_next = lax.psum(exact_dot(merged.T, p_hat), ('dp', 'fsdp')) / groups]
    all_gather x1, waiting for transfers between devices: 19.6 us -> 79.4 us  [per_device(): lax.all_gather(weight, 'fsdp', axis=0, tiled=True)]
    psum x1 -> x0, blocking collectives: 54.5 us -> none  [per_device(): gram_sum = lax.psum(gram_part, 'fsdp')]
    pallas_call x0 -> x1, Pallas kernels: none -> 49.6 us  [tail(): pl.pallas_call(functools.partial(tail_kernel, grad_scale), out_shape=(jax...]
    reduce_scatter x1, waiting for transfers between devices: 178 us -> 149 us  [per_device(): lax.psum_scatter(lax.dot_general(tokens, cotangent, (((0,), (0,)), ((), (...]
    dot_general x4 -> x0, matrix products: 13.6 us -> none  [exact_dot(): jnp.dot(left, right, precision=highest, preferred_element_type=jnp.float32)]
    another operation x5 -> x0, other arithmetic: 12.1 us -> none  [the longest x3 6.52 us: per_device(): lower_factor = jnp.linalg.cholesky(gram_sum)]
  transfers between devices with their start and end apart: 4 -> 2, of which waited for: 4 -> 2; matrix products, arithmetic and copies ran while one was open for 9% -> 13% of each run, Pallas kernels for 0% -> 0%
where the time goes in v1:
time: 343 us; the launch traced here: 342 us
  waiting for transfers between devices  229 us (67%)
  Pallas kernels  49.6 us (14%)
  matrix products  45.5 us (13%)
  between operations  14.1 us (4%)
  local copies, waits for them, and re-layouts  3.7 us (1%)
    reduce_scatter x1, waiting for transfers between devices, per_device(): lax.psum_scatter(lax.dot_general(tokens, cotangent, (((0,), (0,)), ((), (...  149 us
    all_gather x1, waiting for transfers between devices, per_device(): lax.all_gather(weight, 'fsdp', axis=0, tiled=True)  79.4 us
    pallas_call x1, Pallas kernels, tail(): pl.pallas_call(functools.partial(tail_kernel, grad_scale), out_shape=(jax...  49.6 us
    dot_general x1, matrix products, per_device(): lax.dot_general(cotangent, lax.all_gather(weight, 'fsdp', axis=0, tiled=T...  29.6 us
    dot_general x1, matrix products, per_device(): lax.dot_general(tokens, cotangent, (((0,), (0,)), ((), ())), preferred_el...  15.9 us
  transfers between devices with their start and end apart: 2, of which 2 were waited for; matrix products, arithmetic and copies ran while one was open for 13% of the time, Pallas kernels for 0%

profile of v1, /device:TPU:0, one launch (start us, length us, event | category | flops | bytes accessed | tf_op | source)
XLA Modules:
  0.0 342.4 jit_solution(2123993747698955549)
XLA Ops:
  7.2 0.0 copy-start
  7.2 0.0 all-gather.2.cloned.1.call-start
  7.2 0.7 all-gather.2.cloned.1.call-update
  7.9 0.0 reduce-scatter.2.cloned.1.call-start
  8.0 0.4 copy-done
  8.4 15.9 %convolution_convert_fusion = bf16[8192,1024]{1,0:T(8,128)(2,1)} fusion(bf16[512,8192]{1,0:T(8,128)(2,1)} %param.5, bf16[512,1024]{1,0:T(8,128)(2,1)S(1)} %copy-done), kind=kOutput, calls=%fused_computation | convolution fusion | flops 8598323200 | bytes 26214400 | tf_op jit(solution)/shard_map/dot_general | solution.py:189
  24.3 0.0 reduce-scatter.2.cloned.1.call-update
  24.3 0.0 copy-start.1
  24.4 0.0 copy-start.3
  24.4 79.4 %all-gather.2.cloned.1.call-done = bf16[8192,1024]{1,0:T(8,128)(2,1)} async-done(((bf16[512,1024]{1,0:T(8,128)(2,1)}), bf16[8192,1024]{1,0:T(8,128)(2,1)}) %all-gather.2.cloned.1.call-update) | async-done | bytes 16777232 | tf_op jit(solution)/shard_map/all_gather | solution.py:183
  103.8 29.6 %convolution_convert_fusion.1 = bf16[512,8192]{1,0:T(8,128)(2,1)} fusion(bf16[512,1024]{1,0:T(8,128)(2,1)S(1)} %copy-done, bf16[8192,1024]{1,0:T(8,128)(2,1)} %all-gather.2.cloned.1.call-done), kind=kOutput, calls=%fused_computation.1 | convolution fusion | flops 8594128896 | bytes 26214400 | tf_op jit(solution)/shard_map/dot_general | solution.py:181
  133.4 149.3 %reduce-scatter.2.cloned.1.call-done.grad_ref = bf16[512,1024]{1,0:T(8,128)(2,1)} async-done(((bf16[8192,1024]{1,0:T(8,128)(2,1)}), bf16[512,1024]{1,0:T(8,128)(2,1)}) %reduce-scatter.2.cloned.1.call-update) | async-done | bytes 1048592 | tf_op jit(solution)/shard_map/reduce_scatter | solution.py:188
  282.7 0.0 copy-done.1
  282.7 0.0 copy-done.3
  282.7 0.0 copy-start.2
  282.7 1.2 copy-done.2
  283.9 49.6 %tail.1 = (f32[64,1024]{1,0:T(8,128)S(1)}, f32[512,1024]{1,0:T(8,128)S(1)}) custom-call(f32[512,1024]{1,0:T(8,128)S(1)} %bitcast.9, bf16[512,1024]{1,0:T(8,128)(2,1)S(1)} %copy-done.2, f32[64,1024]{1,0:T(8,128)S(1)} %bitcast.11), custom_call_target="tpu_custom_call" | custom-call | tf_op jit(solution)/shard_map/tail/pallas_call | solution.py:152
  333.6 0.7 copy.10
  334.3 1.3 copy.11
Async XLA Ops:
  7.2 1.2 copy-start
  7.2 96.6 %all-gather.2.cloned.1.call-start = ((), (), s32[]{:S(2)}) async-start(), calls=%async_computation.1 | async-start | bytes 17825792 | tf_op jit(solution)/shard_map/all_gather | solution.py:183
  7.9 274.8 %reduce-scatter.2.cloned.1.call-start = ((), (), s32[]{:S(2)}) async-start(), calls=%async_computation.2 | async-start | bytes 17825792 | tf_op jit(solution)/shard_map/reduce_scatter | solution.py:188
  24.3 258.4 %copy-start.1 = (f32[1,512,1024]{2,1,0:T(8,128)S(1)}, f32[1,512,1024]{2,1,0:T(8,128)}, u32[]{:S(2)}) copy-start(f32[1,512,1024]{2,1,0:T(8,128)} %param.8) | copy-start | bytes 6291460
  24.4 258.4 %copy-start.3 = (f32[1024,64]{0,1:T(8,128)S(1)}, f32[1024,64]{0,1:T(8,128)}, u32[]{:S(2)}) copy-start(f32[1024,64]{0,1:T(8,128)} %param.9) | copy-start | bytes 786436
  282.7 1.2 copy-start.2
Sparse Core Ops, SparseCore 0:
  9.7 94.0 all-gather.1
  106.2 176.4 reduce-scatter.1

commit v2 on v1

--- a/solution.py
+++ b/solution.py
@@ -47,8 +47,8 @@
 
 
 def tail_kernel(
-    grad_scale, feedback_ref, grad_ref, q_ref, qn_ref, fn_ref,
-    merged, p_slots, g_slots, s_out, s1, s2, s3,
+    merged, q_ref, qn_ref, fn_ref,
+    p_slots, g_slots, s_out, s1, s2, s3,
     p_send, p_recv, g_send, g_recv, s1_send, s1_recv, s2_send, s2_recv, s3_send, s3_recv,
 ):
     zh, y, x, zl, c = where_am_i()
@@ -69,7 +69,6 @@
     for target in everyone:
         pl.semaphore_signal(barrier, inc=1, device_id=target, device_id_type=MESH)
 
-    merged[...] = feedback_ref[...] + grad_ref[...].astype(F32) * grad_scale
     p_slots[d] = exact(q_ref[...], merged[...], ((1,), (1,))).astype(BF16)
     pl.semaphore_wait(barrier, len(everyone))
 
@@ -144,21 +143,20 @@
     fn_ref[...] = merged[...] - exact(p_hat, q_next, ((1,), (0,)))
 
 
-def tail(feedback, grad_rows, q_t, grad_scale):
-    rows, width = feedback.shape
+def tail(merged, q_t):
+    rows, width = merged.shape
     rank = q_t.shape[0]
     vmem = pl.BlockSpec(memory_space=pltpu.VMEM)
     dma = pltpu.SemaphoreType.DMA
     return pl.pallas_call(
-        functools.partial(tail_kernel, grad_scale),
+        tail_kernel,
         out_shape=(
             jax.ShapeDtypeStruct((rank, width), F32),
             jax.ShapeDtypeStruct((rows, width), F32),
         ),
-        in_specs=[vmem] * 3,
+        in_specs=[vmem] * 2,
         out_specs=(vmem, vmem),
         scratch_shapes=[
-            pltpu.VMEM((rows, width), F32),
             pltpu.VMEM((8, rank, rows), BF16),
             pltpu.VMEM((16, rank, rank), F32),
             pltpu.VMEM((16, 16, 256), F32),
@@ -172,28 +170,334 @@
             collective_id=1, has_side_effects=True, vmem_limit_bytes=48 * 1024 * 1024
         ),
         name="tail",
-    )(feedback, grad_rows, q_t)
+    )(merged, q_t)
+
+
+ORDER = [(2, 1), (1, 1), (3, 1), (0, 1), (2, 0), (1, 0), (3, 0), (0, 0)]
+SLOT = {relative: o for o, relative in enumerate(ORDER)}
+Y_UP = [(0, 0), (2, 0), (1, 1), (3, 1)]
+Y_DOWN = [(3, 0), (1, 0), (0, 1), (2, 1)]
+N_COPIES = 96
+
+
+class Copies:
+    def __init__(self, send, recv):
+        self.send, self.recv, self.used, self.all = send, recv, 0, {}
+
+    def start(self, name, src, dst, target):
+        copy = pltpu.make_async_remote_copy(
+            src_ref=src,
+            dst_ref=dst,
+            send_sem=self.send.at[self.used],
+            recv_sem=self.recv.at[self.used],
+            device_id=target,
+            device_id_type=MESH,
+        )
+        self.used += 1
+        copy.start()
+        self.all[name] = copy
+
+    def arrived(self, name):
+        self.all[name].wait_recv()
+
+    def finish(self):
+        for copy in self.all.values():
+            copy.wait_send()
+
+
+def grads_kernel(
+    grad_scale, tokens, cotangent, weight, feedback, input_grad, merged,
+    tok, cot, part, hop, side, z_last, z_send, z_first, w_all, staged,
+    send, recv, load_sem, store_sem,
+):
+    zh, y, x, zl, c = where_am_i()
+    half = y % 2
+    mate = device(zh, y, x, zl, 1 - c)
+    x_up, x_down = device(zh, y, (x + 1) % 4, zl, c), device(zh, y, (x + 3) % 4, zl, c)
+    y_up, y_down = device(zh, (y + 1) % 4, x, zl, c), device(zh, (y + 3) % 4, x, zl, c)
+    z_pair, z_across = device(zh, y, x, 1 - zl, c), device(1 - zh, y, x, 1 - zl, c)
+    partners = [mate, x_up, x_down, y_up, y_down, z_pair, z_across]
+
+    def first_row(relative, core):
+        rx, rz = relative
+        return (((x + rx) % 4) * 4 + ((zl + rz) % 2) * 2 + core) * 512
+
+    barrier = pltpu.get_barrier_semaphore()
+    for target in partners:
+        pl.semaphore_signal(barrier, inc=1, device_id=target, device_id_type=MESH)
+    loads = [pltpu.make_async_copy(cotangent, cot.at[0:512], load_sem.at[8])]
+    for o, relative in enumerate(ORDER):
+        columns = pl.ds(pl.multiple_of(first_row(relative, c), 512), 512)
+        loads.append(pltpu.make_async_copy(tokens.at[:, columns], tok.at[o, 0:512], load_sem.at[o]))
+    for load in loads:
+        load.start()
+    pl.semaphore_wait(barrier, len(partners))
+
+    go = Copies(send, recv)
+    go.start("cot", cotangent, cot.at[512:1024], mate)
+    for o, relative in enumerate(ORDER):
+        columns = pl.ds(pl.multiple_of(first_row(relative, 1 - c), 512), 512)
+        go.start(("tok", o), tokens.at[:, columns], tok.at[o, 512:1024], mate)
+
+    my_half = weight.at[pl.ds(pl.multiple_of(half * 256, 256), 256)]
+    own_half = pltpu.make_async_copy(my_half, w_all.at[SLOT[0, 0], 0], load_sem.at[9])
+    own_half.start()
+    go.start(("wx", 3), my_half, w_all.at[SLOT[3, 0], 0], x_up)
+    go.start(("wx", 1), my_half, w_all.at[SLOT[1, 0], 0], x_down)
+    go.start(("wz", 0), my_half, w_all.at[SLOT[0, 1], 0], z_across)
+    go.start(("wy", (0, 0)), my_half, w_all.at[SLOT[0, 0], 1], y_up)
+
+    def weight_y(relative):
+        target = y_up if relative in Y_UP else y_down
+        go.start(("wy", relative), w_all.at[SLOT[relative], 0], w_all.at[SLOT[relative], 1], target)
+
+    def weight_x():
+        go.arrived(("wx", 3))
+        go.start(("wf", 0), w_all.at[SLOT[3, 0], 0, 0:128], w_all.at[SLOT[2, 0], 0, 0:128], x_up)
+        go.start(("wz", 3), w_all.at[SLOT[3, 0], 0], w_all.at[SLOT[3, 1], 0], z_across)
+        weight_y((3, 0))
+        go.arrived(("wx", 1))
+        go.start(("wf", 1), w_all.at[SLOT[1, 0], 0, 128:256], w_all.at[SLOT[2, 0], 0, 128:256], x_down)
+        go.start(("wz", 1), w_all.at[SLOT[1, 0], 0], w_all.at[SLOT[1, 1], 0], z_across)
+        weight_y((1, 0))
+
+    def weight_opposite():
+        go.arrived(("wf", 0))
+        go.arrived(("wf", 1))
+        go.start(("wz", 2), w_all.at[SLOT[2, 0], 0], w_all.at[SLOT[2, 1], 0], z_across)
+        weight_y((2, 0))
+
+    def weight_z(rx):
+        go.arrived(("wz", rx))
+        weight_y((rx, 1))
+
+    stores = []
+
+    def project(relative, which):
+        n = len(stores)
+        slot = SLOT[relative]
+
+        @pl.loop(0, 4)
+        def _(i):
+            rows = pl.ds(pl.multiple_of(i * 256, 256), 256)
+            staged[n, rows] = lax.dot_general(
+                cot[rows], w_all[slot, which], (((1,), (1,)), ((), ())), preferred_element_type=F32
+            ).astype(BF16)
+
+        column = first_row(relative, c) + (half if which == 0 else 1 - half) * 256
+        columns = pl.ds(pl.multiple_of(column, 256), 256)
+        store = pltpu.make_async_copy(staged.at[n, 0:512], input_grad.at[:, columns], store_sem.at[n])
+        store.start()
+        stores.append(store)
+        go.start(("out", n), staged.at[n, 512:1024], input_grad.at[:, columns], mate)
+
+    def project_y(relative):
+        go.arrived(("wy", relative))
+        project(relative, 1)
+
+    def partial(o):
+        loads[1 + o].wait()
+        go.arrived(("tok", o))
+
+        @pl.loop(0, 2)
+        def _(i):
+            rows = pl.ds(pl.multiple_of(i * 256, 256), 256)
+            part[o, rows] = lax.dot_general(
+                tok[o, :, rows], cot[...], (((0,), (0,)), ((), ())), preferred_element_type=F32
+            ).astype(BF16)
+
+    START = [0, 0, 512]
+    ACROSS = [1, 0, 0]
+
+    def columns_of(s, which):
+        return pl.ds(START[s] + 256 * which, 256)
+
+    def opposite(s):
+        src = part.at[SLOT[2, ACROSS[s]]]
+        go.start(("hop", s, 0), src.at[:, columns_of(s, 0)], hop.at[s, 0], x_up)
+        go.start(("hop", s, 1), src.at[:, columns_of(s, 1)], hop.at[s, 1], x_down)
+
+    def beside_up(s):
+        src = part.at[SLOT[1, ACROSS[s]]]
+        go.start(("side", s, 0, 1), src.at[:, columns_of(s, 1)], side.at[s, 0, :, 256:512], x_up)
+
+    def beside_down(s):
+        src = part.at[SLOT[3, ACROSS[s]]]
+        go.start(("side", s, 1, 0), src.at[:, columns_of(s, 0)], side.at[s, 1, :, 0:256], x_down)
+
+    def add_into(dst, dst_columns, src, src_columns):
+        @pl.loop(0, 4)
+        def _(i):
+            rows = pl.ds(pl.multiple_of(i * 128, 128), 128)
+            dst[rows, dst_columns] = (
+                dst[rows, dst_columns].astype(F32) + src[rows, src_columns].astype(F32)
+            ).astype(BF16)
+
+    def pass_on(s):
+        for which, rx, target in ((0, 1, x_up), (1, 3, x_down)):
+            go.arrived(("hop", s, which))
+            mine = part.at[SLOT[rx, ACROSS[s]]]
+            add_into(mine, columns_of(s, which), hop.at[s, which], pl.ds(0, 256))
+            go.start(
+                ("side", s, which, which), mine.at[:, columns_of(s, which)],
+                side.at[s, which, :, 256 * which : 256 * which + 256], target,
+            )
+
+    def sides_arrived(s):
+        for which in range(2):
+            for columns in range(2):
+                go.arrived(("side", s, which, columns))
+
+    def z_exchange(rx):
+        go.start(("z1", rx), part.at[SLOT[rx, 1], :, 512:1024], z_first.at[rx], z_pair)
+
+    def z_sum(rx):
+        go.arrived(("z1", rx))
+        add_into(part.at[SLOT[rx, 0]], pl.ds(512, 512), z_first.at[rx], pl.ds(0, 512))
+
+    def finish_across():
+        sides_arrived(0)
+
+        @pl.loop(0, 4)
+        def _(i):
+            rows = pl.ds(pl.multiple_of(i * 128, 128), 128)
+            z_send[rows] = (
+                part[SLOT[0, 1], rows, 0:512].astype(F32)
+                + side[0, 0, rows].astype(F32)
+                + side[0, 1, rows].astype(F32)
+            ).astype(BF16)
+
+        go.start("z2", z_send, z_last, z_pair)
+
+    def finish_here():
+        sides_arrived(1)
+        go.arrived("z2")
+
+        @pl.loop(0, 4)
+        def _(i):
+            rows = pl.ds(pl.multiple_of(i * 128, 128), 128)
+            total = (
+                part[SLOT[0, 0], rows, 0:512].astype(F32)
+                + side[1, 0, rows].astype(F32)
+                + side[1, 1, rows].astype(F32)
+                + z_last[rows].astype(F32)
+            )
+            merged[rows, 0:512] = feedback[rows, 0:512] + total * grad_scale
+
+    def finish_second():
+        sides_arrived(2)
+        go.arrived(("z1", 0))
+
+        @pl.loop(0, 4)
+        def _(i):
+            rows = pl.ds(pl.multiple_of(i * 128, 128), 128)
+            total = (
+                part[SLOT[0, 0], rows, 512:1024].astype(F32)
+                + side[2, 0, rows].astype(F32)
+                + side[2, 1, rows].astype(F32)
+                + z_first[0, rows].astype(F32)
+            )
+            merged[rows, 512:1024] = feedback[rows, 512:1024] + total * grad_scale
+
+    loads[0].wait()
+    go.arrived("cot")
+    partial(0)
+    opposite(0)
+    z_exchange(2)
+    partial(1)
+    beside_up(0)
+    z_exchange(1)
+    partial(2)
+    beside_down(0)
+    z_exchange(3)
+    partial(3)
+    z_exchange(0)
+    partial(4)
+    opposite(1)
+    partial(5)
+    beside_up(1)
+    partial(6)
+    beside_down(1)
+    pass_on(0)
+    partial(7)
+    weight_x()
+    own_half.wait()
+    project((0, 0), 0)
+    project_y((0, 0))
+    z_sum(2)
+    opposite(2)
+    weight_z(0)
+    project((0, 1), 0)
+    project((3, 0), 0)
+    pass_on(1)
+    weight_opposite()
+    project((1, 0), 0)
+    z_sum(1)
+    beside_up(2)
+    project((2, 0), 0)
+    weight_z(3)
+    finish_across()
+    project((3, 1), 0)
+    project_y((3, 0))
+    weight_z(1)
+    z_sum(3)
+    beside_down(2)
+    project((1, 1), 0)
+    pass_on(2)
+    project_y((1, 0))
+    weight_z(2)
+    project((2, 1), 0)
+    project_y((2, 0))
+    project_y((0, 1))
+    project_y((3, 1))
+    finish_here()
+    project_y((1, 1))
+    project_y((2, 1))
+    finish_second()
+    for n in range(16):
+        go.arrived(("out", n))
+        stores[n].wait()
+    go.finish()
+
+
+def grads(tokens, cotangent, weight, feedback, grad_scale):
+    rows, width = feedback.shape
+    vmem = pl.BlockSpec(memory_space=pltpu.VMEM)
+    hbm = pl.BlockSpec(memory_space=pl.ANY)
+    dma = pltpu.SemaphoreType.DMA
+    return pl.pallas_call(
+        functools.partial(grads_kernel, grad_scale),
+        out_shape=(
+            jax.ShapeDtypeStruct(tokens.shape, BF16),
+            jax.ShapeDtypeStruct((rows, width), F32),
+        ),
+        in_specs=[hbm, hbm, hbm, vmem],
+        out_specs=(hbm, vmem),
+        scratch_shapes=[
+            pltpu.VMEM((8, 1024, 512), BF16),
+            pltpu.VMEM((1024, 1024), BF16),
+            pltpu.VMEM((8, 512, 1024), BF16),
+            pltpu.VMEM((3, 2, 512, 256), BF16),
+            pltpu.VMEM((3, 2, 512, 512), BF16),
+            pltpu.VMEM((512, 512), BF16),
+            pltpu.VMEM((512, 512), BF16),
+            pltpu.VMEM((4, 512, 512), BF16),
+            pltpu.VMEM((8, 2, 256, 1024), BF16),
+            pltpu.VMEM((16, 1024, 256), BF16),
+            dma((N_COPIES,)), dma((N_COPIES,)), dma((10,)), dma((16,)),
+        ],
+        compiler_params=pltpu.CompilerParams(
+            collective_id=2, has_side_effects=True, vmem_limit_bytes=60 * 1024 * 1024
+        ),
+        name="grads",
+    )(tokens, cotangent, weight, feedback)
 
 
 def per_device(tokens, cotangent, weight, feedback, q_factor):
     members = lax.axis_size("fsdp")
     grad_scale = 1.0 / math.sqrt(tokens.shape[0] * members)
-    product = lax.dot_general(
-        cotangent,
-        lax.all_gather(weight, "fsdp", axis=0, tiled=True),
-        (((1,), (1,)), ((), ())),
-        preferred_element_type=F32,
-    )
-    input_grad = product.astype(BF16)
-    grad_rows = lax.psum_scatter(
-        lax.dot_general(
-            tokens, cotangent, (((0,), (0,)), ((), ())), preferred_element_type=F32
-        ).astype(BF16),
-        "fsdp",
-        scatter_dimension=0,
-        tiled=True,
-    )
-    q_next, feedback_next = tail(feedback[0], grad_rows, q_factor.T, grad_scale)
+    input_grad, merged = grads(tokens, cotangent, weight, feedback[0], grad_scale)
+    q_next, feedback_next = tail(merged, q_factor.T)
     return (input_grad, q_next.T, feedback_next[None])
 
 

time: 343 us -> 153 us (0.45)
  waiting for transfers between devices: 229 us -> 0 us
  Pallas kernels: 49.6 us -> 140 us
  matrix products: 45.5 us -> 0 us
  between operations: 14.1 us -> 0.67 us
  local copies, waits for them, and re-layouts: 3.7 us -> 11.4 us
    reduce_scatter x1 -> x0, waiting for transfers between devices: 149 us -> none  [per_device(): lax.psum_scatter(lax.dot_general(tokens, cotangent, (((0,), (0,)), ((), (...]
    pallas_call x1 -> x2, Pallas kernels: 49.6 us -> 140 us  [the longest x1 98 us: grads(): pl.pallas_call(functools.partial(grads_kernel, grad_scale), out_shape=(ja...]
    all_gather x1 -> x0, waiting for transfers between devices: 79.4 us -> none  [per_device(): lax.all_gather(weight, 'fsdp', axis=0, tiled=True)]
    dot_general x2 -> x0, matrix products: 45.5 us -> none  [the longest x1 29.6 us: per_device(): lax.dot_general(cotangent, lax.all_gather(weight, 'fsdp', axis=0, tiled=T...]
    unnamed x10 -> x7, local copies, waits for them, and re-layouts: 3.7 us -> 11.4 us
  transfers between devices with their start and end apart: 2 -> 0, of which waited for: 2 -> 0; matrix products, arithmetic and copies ran while one was open for 13% -> 0% of each run, Pallas kernels for 0% -> 0%
where the time goes in v2:
time: 153 us; the launch traced here: 152 us
  Pallas kernels  140 us (92%)
  local copies, waits for them, and re-layouts  11.4 us (7%)
    pallas_call x1, Pallas kernels, grads(): pl.pallas_call(functools.partial(grads_kernel, grad_scale), out_shape=(ja...  98 us
    pallas_call x1, Pallas kernels, tail(): pl.pallas_call(tail_kernel, out_shape=(jax.ShapeDtypeStruct((rank, width)...  42.2 us
    unnamed x7, local copies, waits for them, and re-layouts  11.4 us

profile of v2, /device:TPU:0, one launch (start us, length us, event | category | flops | bytes accessed | tf_op | source)
XLA Modules:
  0.0 152.3 jit_solution(6010275774573585804)
XLA Ops:
  0.6 0.0 copy-start.1
  0.6 98.0 %grads.1 = (bf16[512,8192]{1,0:T(8,128)(2,1)}, f32[512,1024]{1,0:T(8,128)}) custom-call(bf16[512,8192]{1,0:T(8,128)(2,1)} %tokens.1, bf16[512,1024]{1,0:T(8,128)(2,1)} %cotangent.1, bf16[512,1024]{1,0:T(8,128)(2,1)} %weight.1, f32[512,1024]{1,0:T(8,128)} %bitcast.7), custom_call_target="tpu_custom_call" | custom-call | tf_op jit(solution)/shard_map/grads/pallas_call | solution.py:468
  98.7 0.0 copy-done.1
  98.7 0.0 copy-start
  98.7 1.6 %copy-done = f32[512,1024]{1,0:T(8,128)S(1)} copy-done((f32[512,1024]{1,0:T(8,128)S(1)}, f32[512,1024]{1,0:T(8,128)}, u32[]{:S(2)}) %copy-start) | copy-done | bytes 2097176
  100.3 42.2 %tail.1 = (f32[64,1024]{1,0:T(8,128)S(1)}, f32[512,1024]{1,0:T(8,128)S(1)}) custom-call(f32[512,1024]{1,0:T(8,128)S(1)} %copy-done, f32[64,1024]{1,0:T(8,128)S(1)} %bitcast.5), custom_call_target="tpu_custom_call" | custom-call | tf_op jit(solution)/shard_map/tail/pallas_call | solution.py:151
  142.5 7.8 %copy.11 = bf16[512,8192]{1,0:T(8,128)(2,1)} copy(bf16[512,8192]{1,0:T(8,128)(2,1)} %get-tuple-element.14) | data formatting | bytes 16777216
  150.3 0.7 copy.12
  151.0 1.3 copy.13
Async XLA Ops:
  0.6 98.0 %copy-start.1 = (f32[1024,64]{0,1:T(8,128)S(1)}, f32[1024,64]{0,1:T(8,128)}, u32[]{:S(2)}) copy-start(f32[1024,64]{0,1:T(8,128)} %param.9) | copy-start | bytes 786436
  98.7 1.6 %copy-start = (f32[512,1024]{1,0:T(8,128)S(1)}, f32[512,1024]{1,0:T(8,128)}, u32[]{:S(2)}) copy-start(f32[512,1024]{1,0:T(8,128)} %get-tuple-element.8.merged) | copy-start | bytes 6291460

commit v3 on v2

--- a/solution.py
+++ b/solution.py
@@ -28,156 +28,48 @@
     return lax.dot_general(left, right, (dims, ((), ())), precision=HIGHEST, preferred_element_type=F32)
 
 
-def spread(src, slots, send_sem, recv_sem, me, targets):
-    copies = []
+def spread(copies, name, src, slots, me, targets):
     for k, target in enumerate(targets):
-        copies.append(
-            pltpu.make_async_remote_copy(
-                src_ref=src(k),
-                dst_ref=slots.at[me],
-                send_sem=send_sem.at[k],
-                recv_sem=recv_sem.at[k],
-                device_id=target,
-                device_id_type=MESH,
-            )
-        )
-    for copy in copies:
-        copy.start()
-    return copies
-
-
-def tail_kernel(
-    merged, q_ref, qn_ref, fn_ref,
-    p_slots, g_slots, s_out, s1, s2, s3,
-    p_send, p_recv, g_send, g_recv, s1_send, s1_recv, s2_send, s2_recv, s3_send, s3_recv,
-):
-    zh, y, x, zl, c = where_am_i()
-    d = lax.axis_index("dp")
-    f = lax.axis_index("fsdp")
-    plane = x * 4 + y
-    column = zh * 4 + zl * 2 + c
-
-    group_of = [((d + k) % 8, f) for k in range(1, 8)]
-    member_of = [(d, (f + k) % 16) for k in range(1, 16)]
-    plane_at = [(plane + k) % 16 for k in range(1, 16)]
-    plane_of = [device(zh, t % 4, t // 4, zl, c) for t in plane_at]
-    column_at = [(column + k) % 8 for k in range(1, 8)]
-    column_of = [device(t // 4, y, x, (t // 2) % 2, t % 2) for t in column_at]
-
-    barrier = pltpu.get_barrier_semaphore()
-    everyone = group_of + member_of + plane_of + column_of
-    for target in everyone:
-        pl.semaphore_signal(barrier, inc=1, device_id=target, device_id_type=MESH)
-
-    p_slots[d] = exact(q_ref[...], merged[...], ((1,), (1,))).astype(BF16)
-    pl.semaphore_wait(barrier, len(everyone))
-
-    copies = spread(lambda k: p_slots.at[d], p_slots, p_send, p_recv, d, group_of)
-    for copy in copies:
-        copy.wait()
-    total = p_slots[0].astype(F32)
-    for k in range(1, 8):
-        total = total + p_slots[k].astype(F32)
-    factor = total * 0.125
-
-    s_local = exact(factor, merged[...], ((1,), (0,))) * 0.125
-    for i in range(4):
-        for j in range(4):
-            s_out[i * 4 + j] = s_local[16 * i : 16 * i + 16, 256 * j : 256 * j + 256]
-    s1_copies = spread(lambda k: s_out.at[plane_at[k]], s1, s1_send, s1_recv, plane, plane_of)
-    g_slots[f] = exact(factor, factor, ((1,), (1,)))
-    g_copies = spread(lambda k: g_slots.at[f], g_slots, g_send, g_recv, f, member_of)
-    s1[plane] = s_out[plane]
-    for copy in s1_copies:
-        copy.wait()
-    part = s1[0]
-    for k in range(1, 16):
-        part = part + s1[k]
-    s2[column] = part
-    s2_copies = spread(lambda k: s2.at[column], s2, s2_send, s2_recv, column, column_of)
-
-    for copy in g_copies:
-        copy.wait()
-    gram = g_slots[0]
-    for k in range(1, 16):
-        gram = gram + g_slots[k]
-    row_id = lax.broadcasted_iota(jnp.int32, (64, 64), 0)
-    lane_id = lax.broadcasted_iota(jnp.int32, (64, 64), 1)
-    eye = jnp.where(row_id == lane_id, 1.0, 0.0).astype(F32)
-    work = jnp.concatenate([eye, gram], axis=1)
-    rows = lax.broadcasted_iota(jnp.int32, (64, 128), 0)
-
-    def eliminate(work, k):
-        pivot = jnp.broadcast_to(work[k : k + 1, 64 + k : 65 + k], (64, 128))
-        column_k = jnp.broadcast_to(work[:, 64 + k : 65 + k], (64, 128))
-        row_k = jnp.broadcast_to(work[k : k + 1, :], (64, 128))
-        root = lax.rsqrt(pivot)
-        root = root * (1.5 - 0.5 * pivot * root * root)
-        scaled = row_k * root
-        below = work - (column_k * root) * scaled
-        return jnp.where(rows > k, below, jnp.where(rows == k, scaled, work))
-
-    for k in range(16):
-        work = eliminate(work, k)
-
-    for copy in s2_copies:
-        copy.wait()
-    part = s2[0]
-    for k in range(1, 8):
-        part = part + s2[k]
-    s3[plane] = part
-    s3_copies = spread(lambda k: s3.at[plane], s3, s3_send, s3_recv, plane, plane_of)
-
-    for k in range(16, 64):
-        work = eliminate(work, k)
-    inverse = work[:, :64]
-    p_hat = jnp.transpose(exact(inverse, factor, ((1,), (0,))))
-
-    for copy in s3_copies:
-        copy.wait()
-    s_total = jnp.concatenate(
-        [jnp.concatenate([s3[i * 4 + j] for j in range(4)], axis=1) for i in range(4)], axis=0
-    )
-    q_next = exact(inverse, s_total, ((1,), (0,)))
-    qn_ref[...] = q_next
-    fn_ref[...] = merged[...] - exact(p_hat, q_next, ((1,), (0,)))
-
-
-def tail(merged, q_t):
-    rows, width = merged.shape
-    rank = q_t.shape[0]
-    vmem = pl.BlockSpec(memory_space=pltpu.VMEM)
-    dma = pltpu.SemaphoreType.DMA
-    return pl.pallas_call(
-        tail_kernel,
-        out_shape=(
-            jax.ShapeDtypeStruct((rank, width), F32),
-            jax.ShapeDtypeStruct((rows, width), F32),
-        ),
-        in_specs=[vmem] * 2,
-        out_specs=(vmem, vmem),
-        scratch_shapes=[
-            pltpu.VMEM((8, rank, rows), BF16),
-            pltpu.VMEM((16, rank, rank), F32),
-            pltpu.VMEM((16, 16, 256), F32),
-            pltpu.VMEM((16, 16, 256), F32),
-            pltpu.VMEM((8, 16, 256), F32),
-            pltpu.VMEM((16, 16, 256), F32),
-            dma((7,)), dma((7,)), dma((15,)), dma((15,)), dma((15,)), dma((15,)),
-            dma((7,)), dma((7,)), dma((15,)), dma((15,)),
-        ],
-        compiler_params=pltpu.CompilerParams(
-            collective_id=1, has_side_effects=True, vmem_limit_bytes=48 * 1024 * 1024
-        ),
-        name="tail",
-    )(merged, q_t)
+        copies.start((name, k), src(k), slots.at[me], target)
+
+
+def gathered(copies, name, targets):
+    for k in range(len(targets)):
+        copies.arrived((name, k))
+
+
+def total_of(slots, n):
+    total = slots[0].astype(F32)
+    for k in range(1, n):
+        total = total + slots[k].astype(F32)
+    return total
+
+
+def eliminate(work, k, row_id):
+    group, first = k // 8, k % 8
+    columns = [jnp.broadcast_to(work[:, :, 64 + k + j : 65 + k + j], (8, 8, 128)) for j in range(4)]
+    rows = [jnp.broadcast_to(work[group, first + j : first + j + 1, :], (8, 128)) for j in range(4)]
+    pivot = {}
+    for j in range(4):
+        for i in range(j, 4):
+            pivot[i, j] = jnp.broadcast_to(columns[j][group, first + i : first + i + 1, :], (8, 128))
+    for j in range(4):
+        inverse = 1.0 / pivot[j, j]
+        multiplier = columns[j] * inverse
+        for i in range(j + 1, 4):
+            columns[i] = columns[i] - multiplier * pivot[i, j]
+            scale = pivot[i, j] * inverse
+            rows[i] = rows[i] - scale * rows[j]
+            for m in range(i, 4):
+                pivot[m, i] = pivot[m, i] - scale * pivot[m, j]
+        work = work - jnp.where(row_id > k + j, multiplier, 0.0) * rows[j]
+    return work
 
 
 ORDER = [(2, 1), (1, 1), (3, 1), (0, 1), (2, 0), (1, 0), (3, 0), (0, 0)]
 SLOT = {relative: o for o, relative in enumerate(ORDER)}
-Y_UP = [(0, 0), (2, 0), (1, 1), (3, 1)]
-Y_DOWN = [(3, 0), (1, 0), (0, 1), (2, 1)]
-N_COPIES = 96
+Y_UP = [(0, 0), (3, 0), (2, 0), (1, 1)]
+N_COPIES = 144
 
 
 class Copies:
@@ -205,9 +97,10 @@
             copy.wait_send()
 
 
-def grads_kernel(
-    grad_scale, tokens, cotangent, weight, feedback, input_grad, merged,
-    tok, cot, part, hop, side, z_last, z_send, z_first, w_all, staged,
+def step_kernel(
+    grad_scale, tokens, cotangent, weight, feedback, q_ref, input_grad, merged, p_hat_ref, q_next_ref,
+    tok, cot, part, hop, side, z_last, z_send, z_first, w_all,
+    pa_slots, pb_slots, g_slots, s_out, s1, s2, s3,
     send, recv, load_sem, store_sem,
 ):
     zh, y, x, zl, c = where_am_i()
@@ -216,7 +109,19 @@
     x_up, x_down = device(zh, y, (x + 1) % 4, zl, c), device(zh, y, (x + 3) % 4, zl, c)
     y_up, y_down = device(zh, (y + 1) % 4, x, zl, c), device(zh, (y + 3) % 4, x, zl, c)
     z_pair, z_across = device(zh, y, x, 1 - zl, c), device(1 - zh, y, x, 1 - zl, c)
+    d = lax.axis_index("dp")
+    f = lax.axis_index("fsdp")
+    plane = x * 4 + y
+    column = zh * 4 + zl * 2 + c
+    y_of = [device(zh, (y + k) % 4, x, zl, c) for k in range(1, 4)]
+    z_of = [device(1 - zh, y, x, zl, c)]
+    member_of = [(d, (f + k) % 16) for k in range(1, 16)]
+    plane_at = [(plane + k) % 16 for k in range(1, 16)]
+    plane_of = [device(zh, t % 4, t // 4, zl, c) for t in plane_at]
+    column_at = [(column + k) % 8 for k in range(1, 8)]
+    column_of = [device(t // 4, y, x, (t // 2) % 2, t % 2) for t in column_at]
     partners = [mate, x_up, x_down, y_up, y_down, z_pair, z_across]
+    partners = partners + y_of + z_of + member_of + plane_of + column_of
 
     def first_row(relative, core):
         rx, rz = relative
@@ -280,16 +185,17 @@
         @pl.loop(0, 4)
         def _(i):
             rows = pl.ds(pl.multiple_of(i * 256, 256), 256)
-            staged[n, rows] = lax.dot_general(
+            tok[slot, rows, 256 * which : 256 * which + 256] = lax.dot_general(
                 cot[rows], w_all[slot, which], (((1,), (1,)), ((), ())), preferred_element_type=F32
             ).astype(BF16)
 
         column = first_row(relative, c) + (half if which == 0 else 1 - half) * 256
         columns = pl.ds(pl.multiple_of(column, 256), 256)
-        store = pltpu.make_async_copy(staged.at[n, 0:512], input_grad.at[:, columns], store_sem.at[n])
+        made = tok.at[slot, :, 256 * which : 256 * which + 256]
+        store = pltpu.make_async_copy(made.at[0:512], input_grad.at[:, columns], store_sem.at[n])
         store.start()
         stores.append(store)
-        go.start(("out", n), staged.at[n, 512:1024], input_grad.at[:, columns], mate)
+        go.start(("out", n), made.at[512:1024], input_grad.at[:, columns], mate)
 
     def project_y(relative):
         go.arrived(("wy", relative))
@@ -412,67 +318,118 @@
     z_exchange(3)
     partial(3)
     z_exchange(0)
+    weight_x()
     partial(4)
     opposite(1)
+    weight_z(0)
     partial(5)
     beside_up(1)
+    pass_on(0)
     partial(6)
     beside_down(1)
-    pass_on(0)
+    z_sum(2)
+    opposite(2)
     partial(7)
-    weight_x()
     own_half.wait()
     project((0, 0), 0)
     project_y((0, 0))
-    z_sum(2)
-    opposite(2)
-    weight_z(0)
     project((0, 1), 0)
+    weight_z(3)
     project((3, 0), 0)
-    pass_on(1)
+    project((1, 0), 0)
     weight_opposite()
-    project((1, 0), 0)
     z_sum(1)
     beside_up(2)
+    project((3, 1), 0)
     project((2, 0), 0)
-    weight_z(3)
+    pass_on(1)
+    weight_z(1)
+    project((1, 1), 0)
     finish_across()
-    project((3, 1), 0)
-    project_y((3, 0))
-    weight_z(1)
     z_sum(3)
     beside_down(2)
-    project((1, 1), 0)
-    pass_on(2)
+    project_y((3, 0))
     project_y((1, 0))
     weight_z(2)
     project((2, 1), 0)
+    pass_on(2)
+    project_y((0, 1))
     project_y((2, 0))
-    project_y((0, 1))
+    finish_here()
+    p_local = exact(q_ref[:, 0:512], merged[:, 0:512], ((1,), (1,)))
+    finish_second()
+    p_local = p_local + exact(q_ref[:, 512:1024], merged[:, 512:1024], ((1,), (1,)))
+    pa_slots[y] = p_local.astype(BF16)
+    spread(go, "pa", lambda k: pa_slots.at[y], pa_slots, y, y_of)
     project_y((3, 1))
-    finish_here()
     project_y((1, 1))
+    gathered(go, "pa", y_of)
+    pb_slots[zh] = total_of(pa_slots, 4).astype(BF16)
+    spread(go, "pb", lambda k: pb_slots.at[zh], pb_slots, zh, z_of)
     project_y((2, 1))
-    finish_second()
+    gathered(go, "pb", z_of)
+    factor = total_of(pb_slots, 2) * 0.125
+
+    g_slots[f] = exact(factor, factor, ((1,), (1,)))
+    spread(go, "gram", lambda k: g_slots.at[f], g_slots, f, member_of)
+    s_local = exact(factor, merged[...], ((1,), (0,))) * 0.125
+    for i in range(4):
+        for j in range(4):
+            s_out[i * 4 + j] = s_local[16 * i : 16 * i + 16, 256 * j : 256 * j + 256]
+    spread(go, "s1", lambda k: s_out.at[plane_at[k]], s1, plane, plane_of)
+    s1[plane] = s_out[plane]
+
+    gathered(go, "gram", member_of)
+    gram = total_of(g_slots, 16)
+    row = lax.broadcasted_iota(jnp.int32, (64, 64), 0)
+    lane = lax.broadcasted_iota(jnp.int32, (64, 64), 1)
+    eye = jnp.where(row == lane, 1.0, 0.0).astype(F32)
+    work = jnp.concatenate([eye, gram], axis=1).reshape(8, 8, 128)
+    row_id = lax.broadcasted_iota(jnp.int32, (8, 8, 128), 0) * 8 + lax.broadcasted_iota(jnp.int32, (8, 8, 128), 1)
+
+    gathered(go, "s1", plane_of)
+    s2[column] = total_of(s1, 16)
+    spread(go, "s2", lambda k: s2.at[column], s2, column, column_of)
+    for k in range(0, 28, 4):
+        work = eliminate(work, k, row_id)
+
+    gathered(go, "s2", column_of)
+    s3[plane] = total_of(s2, 8)
+    spread(go, "s3", lambda k: s3.at[plane], s3, plane, plane_of)
+    for k in range(28, 64, 4):
+        work = eliminate(work, k, row_id)
+    lane_id = lax.broadcasted_iota(jnp.int32, (8, 8, 128), 2)
+    diagonal = jnp.sum(jnp.where(lane_id == row_id + 64, work, 0.0), axis=2, keepdims=True)
+    inverse = (work * (1.0 / jnp.sqrt(diagonal))).reshape(64, 128)[:, :64]
+    p_hat_ref[...] = jnp.transpose(exact(inverse, factor, ((1,), (0,))))
+
     for n in range(16):
         go.arrived(("out", n))
         stores[n].wait()
+    gathered(go, "s3", plane_of)
+    s_total = jnp.concatenate(
+        [jnp.concatenate([s3[i * 4 + j] for j in range(4)], axis=1) for i in range(4)], axis=0
+    )
+    q_next_ref[...] = exact(inverse, s_total, ((1,), (0,)))
     go.finish()
 
 
-def grads(tokens, cotangent, weight, feedback, grad_scale):
+def step(tokens, cotangent, weight, feedback, q_t, grad_scale):
     rows, width = feedback.shape
+    rank = q_t.shape[0]
     vmem = pl.BlockSpec(memory_space=pltpu.VMEM)
     hbm = pl.BlockSpec(memory_space=pl.ANY)
     dma = pltpu.SemaphoreType.DMA
     return pl.pallas_call(
-        functools.partial(grads_kernel, grad_scale),
+        functools.partial(step_kernel, grad_scale),
         out_shape=(
             jax.ShapeDtypeStruct(tokens.shape, BF16),
             jax.ShapeDtypeStruct((rows, width), F32),
+            jax.ShapeDtypeStruct((rows, rank), F32),
+            jax.ShapeDtypeStruct((rank, width), F32),
         ),
-        in_specs=[hbm, hbm, hbm, vmem],
-        out_specs=(hbm, vmem),
+        in_specs=[hbm, hbm, hbm, vmem, vmem],
+        out_specs=(hbm, vmem, vmem, vmem),
         scratch_shapes=[
             pltpu.VMEM((8, 1024, 512), BF16),
             pltpu.VMEM((1024, 1024), BF16),
@@ -483,21 +440,78 @@
             pltpu.VMEM((512, 512), BF16),
             pltpu.VMEM((4, 512, 512), BF16),
             pltpu.VMEM((8, 2, 256, 1024), BF16),
-            pltpu.VMEM((16, 1024, 256), BF16),
+            pltpu.VMEM((4, rank, rows), BF16),
+            pltpu.VMEM((2, rank, rows), BF16),
+            pltpu.VMEM((16, rank, rank), F32),
+            pltpu.VMEM((16, 16, 256), F32),
+            pltpu.VMEM((16, 16, 256), F32),
+            pltpu.VMEM((8, 16, 256), F32),
+            pltpu.VMEM((16, 16, 256), F32),
             dma((N_COPIES,)), dma((N_COPIES,)), dma((10,)), dma((16,)),
         ],
         compiler_params=pltpu.CompilerParams(
             collective_id=2, has_side_effects=True, vmem_limit_bytes=60 * 1024 * 1024
         ),
-        name="grads",
-    )(tokens, cotangent, weight, feedback)
+        name="step",
+    )(tokens, cotangent, weight, feedback, q_t)
+
+
+def results_kernel(made, merged, p_hat, q_next, input_grad, feedback_next, q_out, pieces, wide, read_sem, write_sem):
+    chunk = pieces.shape[1]
+    n = pieces.shape[0]
+    first = pltpu.make_async_copy(merged, wide, read_sem.at[n])
+    first.start()
+    reads, writes = [], []
+    for i in range(n):
+        rows = pl.ds(i * chunk, chunk)
+        reads.append(pltpu.make_async_copy(made.at[rows], pieces.at[i], read_sem.at[i]))
+        writes.append(pltpu.make_async_copy(pieces.at[i], input_grad.at[rows], write_sem.at[i]))
+        reads[i].start()
+    q_out[...] = q_next[...]
+    first.wait()
+    total = wide.shape[0]
+    half = total // 2
+    for h in range(2):
+        rows = pl.ds(h * half, half)
+        wide[rows] = wide[rows] - exact(p_hat[rows], q_next[...], ((1,), (0,)))
+        writes.append(pltpu.make_async_copy(wide.at[rows], feedback_next.at[rows], write_sem.at[n + h]))
+        writes[n + h].start()
+        for i in range(h * n // 2, (h + 1) * n // 2):
+            reads[i].wait()
+            writes[i].start()
+    for write in writes:
+        write.wait()
+
+
+def results(made, merged, p_hat, q_next):
+    n = 8
+    vmem = pl.BlockSpec(memory_space=pltpu.VMEM)
+    hbm = pl.BlockSpec(memory_space=pl.ANY)
+    dma = pltpu.SemaphoreType.DMA
+    return pl.pallas_call(
+        results_kernel,
+        out_shape=(
+            jax.ShapeDtypeStruct(made.shape, BF16),
+            jax.ShapeDtypeStruct(merged.shape, F32),
+            jax.ShapeDtypeStruct(q_next.shape, F32),
+        ),
+        in_specs=[hbm, hbm, vmem, vmem],
+        out_specs=(hbm, hbm, vmem),
+        scratch_shapes=[
+            pltpu.VMEM((n, made.shape[0] // n, made.shape[1]), BF16),
+            pltpu.VMEM(merged.shape, F32),
+            dma((n + 1,)), dma((n + 2,)),
+        ],
+        compiler_params=pltpu.CompilerParams(vmem_limit_bytes=24 * 1024 * 1024),
+        name="results",
+    )(made, merged, p_hat, q_next)
 
 
 def per_device(tokens, cotangent, weight, feedback, q_factor):
     members = lax.axis_size("fsdp")
     grad_scale = 1.0 / math.sqrt(tokens.shape[0] * members)
-    input_grad, merged = grads(tokens, cotangent, weight, feedback[0], grad_scale)
-    q_next, feedback_next = tail(merged, q_factor.T)
+    made, merged, p_hat, q_next = step(tokens, cotangent, weight, feedback[0], q_factor.T, grad_scale)
+    input_grad, feedback_next, q_next = results(made, merged, p_hat, q_next)
     return (input_grad, q_next.T, feedback_next[None])
 
 

time: 153 us -> 133 us (0.87)
  Pallas kernels: 140 us -> 125 us
  local copies, waits for them, and re-layouts: 11.4 us -> 6.86 us
    pallas_call x2, Pallas kernels: 140 us -> 125 us  [the longest x1 119 us: step(): pl.pallas_call(functools.partial(step_kernel, grad_scale), out_shape=(jax...]
    unnamed x7 -> x8, local copies, waits for them, and re-layouts: 11.4 us -> 6.86 us
where the time goes in v3:
time: 133 us
  Pallas kernels  125 us (94%)
  local copies, waits for them, and re-layouts  6.86 us (5%)
    pallas_call x1, Pallas kernels, step(): pl.pallas_call(functools.partial(step_kernel, grad_scale), out_shape=(jax...  119 us
    unnamed x8, local copies, waits for them, and re-layouts  6.86 us
    pallas_call x1, Pallas kernels, results(): pl.pallas_call(results_kernel, out_shape=(jax.ShapeDtypeStruct(made.shape...  6.48 us

profile of v3, /device:TPU:0, one launch (start us, length us, event | category | flops | bytes accessed | tf_op | source)
XLA Modules:
  0.0 132.7 jit_solution(10763592838374748092)
XLA Ops:
  0.6 118.6 %step.1 = (bf16[512,8192]{1,0:T(8,128)(2,1)}, f32[512,1024]{1,0:T(8,128)}, f32[512,64]{1,0:T(8,128)}, f32[64,1024]{1,0:T(8,128)}) custom-call(bf16[512,8192]{1,0:T(8,128)(2,1)} %tokens.1, bf16[512,1024]{1,0:T(8,128)(2,1)} %cotangent.1, bf16[512,1024]{1,0:T(8,128)(2,1)} %weight.1, f32[512,1024]{1,0:T(8,128)} %bitcast.4, f32[64,1024]{1,0:T(8,128)} %bitcast.5), custom_call_target="tpu_custom_call" | custom-call | tf_op jit(solution)/shard_map/step/pallas_call | solution.py:423
  119.2 0.0 copy-start
  119.2 3.4 %copy-done = bf16[512,8192]{1,0:T(8,128)(2,1)S(1)} copy-done((bf16[512,8192]{1,0:T(8,128)(2,1)S(1)}, bf16[512,8192]{1,0:T(8,128)(2,1)}, u32[]{:S(2)}) %copy-start) | copy-done | bytes 8388632
  122.6 0.0 copy-start.1
  122.6 1.6 %copy-done.1 = f32[512,1024]{1,0:T(8,128)S(1)} copy-done((f32[512,1024]{1,0:T(8,128)S(1)}, f32[512,1024]{1,0:T(8,128)}, u32[]{:S(2)}) %copy-start.1) | copy-done | bytes 2097176
  124.2 0.0 copy-start.2
  124.2 0.9 copy-done.2
  125.1 0.0 copy-start.3
  125.1 0.9 copy-done.3
  126.1 6.5 %results.1 = (bf16[512,8192]{1,0:T(8,128)(2,1)}, f32[512,1024]{1,0:T(8,128)}, f32[64,1024]{1,0:T(8,128)}) custom-call(bf16[512,8192]{1,0:T(8,128)(2,1)S(1)} %copy-done, f32[512,1024]{1,0:T(8,128)S(1)} %copy-done.1, f32[512,64]{1,0:T(8,128)S(1)} %copy-done.2, f32[64,1024]{1,0:T(8,128)S(1)} %copy-done.3), custom_call_target="tpu_custom_call" | custom-call | tf_op jit(solution)/shard_map/results/pallas_call | solution.py:491
Async XLA Ops:
  119.2 3.4 %copy-start = (bf16[512,8192]{1,0:T(8,128)(2,1)S(1)}, bf16[512,8192]{1,0:T(8,128)(2,1)}, u32[]{:S(2)}) copy-start(bf16[512,8192]{1,0:T(8,128)(2,1)} %get-tuple-element.10.made) | copy-start | bytes 25165828
  122.6 1.6 %copy-start.1 = (f32[512,1024]{1,0:T(8,128)S(1)}, f32[512,1024]{1,0:T(8,128)}, u32[]{:S(2)}) copy-start(f32[512,1024]{1,0:T(8,128)} %get-tuple-element.11.merged) | copy-start | bytes 6291460
  124.2 0.9 copy-start.2
  125.1 0.9 copy-start.3

commit v4 on v3

--- a/solution.py
+++ b/solution.py
@@ -69,7 +69,7 @@
 ORDER = [(2, 1), (1, 1), (3, 1), (0, 1), (2, 0), (1, 0), (3, 0), (0, 0)]
 SLOT = {relative: o for o, relative in enumerate(ORDER)}
 Y_UP = [(0, 0), (3, 0), (2, 0), (1, 1)]
-N_COPIES = 144
+N_COPIES = 160
 
 
 class Copies:
@@ -98,10 +98,10 @@
 
 
 def step_kernel(
-    grad_scale, tokens, cotangent, weight, feedback, q_ref, input_grad, merged, p_hat_ref, q_next_ref,
+    grad_scale, tokens, cotangent, weight, feedback_in, q_in, input_grad, merged, p_hat_ref, q_next_ref,
     tok, cot, part, hop, side, z_last, z_send, z_first, w_all,
-    pa_slots, pb_slots, g_slots, s_out, s1, s2, s3,
-    send, recv, load_sem, store_sem,
+    pa_slots, pb_slots, g1_slots, g2_slots, wide_factor, s_out, s1, s2, s3_out, s3, met,
+    feedback, q_ref, send, recv, load_sem, store_sem,
 ):
     zh, y, x, zl, c = where_am_i()
     half = y % 2
@@ -115,13 +115,13 @@
     column = zh * 4 + zl * 2 + c
     y_of = [device(zh, (y + k) % 4, x, zl, c) for k in range(1, 4)]
     z_of = [device(1 - zh, y, x, zl, c)]
+    group_of = [((d + k) % 8, f) for k in range(1, 8)]
     member_of = [(d, (f + k) % 16) for k in range(1, 16)]
     plane_at = [(plane + k) % 16 for k in range(1, 16)]
     plane_of = [device(zh, t % 4, t // 4, zl, c) for t in plane_at]
     column_at = [(column + k) % 8 for k in range(1, 8)]
     column_of = [device(t // 4, y, x, (t // 2) % 2, t % 2) for t in column_at]
     partners = [mate, x_up, x_down, y_up, y_down, z_pair, z_across]
-    partners = partners + y_of + z_of + member_of + plane_of + column_of
 
     def first_row(relative, core):
         rx, rz = relative
@@ -134,9 +134,22 @@
     for o, relative in enumerate(ORDER):
         columns = pl.ds(pl.multiple_of(first_row(relative, c), 512), 512)
         loads.append(pltpu.make_async_copy(tokens.at[:, columns], tok.at[o, 0:512], load_sem.at[o]))
-    for load in loads:
+    late = [
+        pltpu.make_async_copy(feedback_in, feedback, load_sem.at[10]),
+        pltpu.make_async_copy(q_in, q_ref, load_sem.at[11]),
+    ]
+    for load in loads + late:
         load.start()
     pl.semaphore_wait(barrier, len(partners))
+
+    rounds = [[x_up, x_down], [y_up, y_down], [y_up, y_down], [z_pair, z_across], [z_pair, z_across], [mate]]
+
+    def meet(n):
+        if n > 0:
+            pl.semaphore_wait(met.at[n - 1], len(rounds[n - 1]))
+        if n < len(rounds):
+            for target in rounds[n]:
+                pl.semaphore_signal(met.at[n], inc=1, device_id=target, device_id_type=MESH)
 
     go = Copies(send, recv)
     go.start("cot", cotangent, cot.at[512:1024], mate)
@@ -244,10 +257,12 @@
             go.arrived(("hop", s, which))
             mine = part.at[SLOT[rx, ACROSS[s]]]
             add_into(mine, columns_of(s, which), hop.at[s, which], pl.ds(0, 256))
-            go.start(
-                ("side", s, which, which), mine.at[:, columns_of(s, which)],
-                side.at[s, which, :, 256 * which : 256 * which + 256], target,
-            )
+            for r in range(2 if s == 2 else 1):
+                rows = pl.ds(256 * r, 256) if s == 2 else pl.ds(0, 512)
+                go.start(
+                    ("side", s, which, which) if s < 2 else ("last", which, r), mine.at[rows, columns_of(s, which)],
+                    side.at[s, which, rows, 256 * which : 256 * which + 256], target,
+                )
 
     def sides_arrived(s):
         for which in range(2):
@@ -290,11 +305,15 @@
             )
             merged[rows, 0:512] = feedback[rows, 0:512] + total * grad_scale
 
-    def finish_second():
-        sides_arrived(2)
-        go.arrived(("z1", 0))
-
-        @pl.loop(0, 4)
+    def finish_second(r):
+        if r == 0:
+            go.arrived(("side", 2, 0, 1))
+            go.arrived(("side", 2, 1, 0))
+            go.arrived(("z1", 0))
+        for which in range(2):
+            go.arrived(("last", which, r))
+
+        @pl.loop(2 * r, 2 * r + 2)
         def _(i):
             rows = pl.ds(pl.multiple_of(i * 128, 128), 128)
             total = (
@@ -308,29 +327,38 @@
     loads[0].wait()
     go.arrived("cot")
     partial(0)
+    meet(0)
     opposite(0)
     z_exchange(2)
     partial(1)
+    meet(1)
     beside_up(0)
     z_exchange(1)
     partial(2)
+    meet(2)
     beside_down(0)
     z_exchange(3)
     partial(3)
+    meet(3)
     z_exchange(0)
     weight_x()
     partial(4)
+    meet(4)
     opposite(1)
     weight_z(0)
     partial(5)
+    meet(5)
     beside_up(1)
     pass_on(0)
     partial(6)
+    meet(6)
     beside_down(1)
     z_sum(2)
     opposite(2)
     partial(7)
     own_half.wait()
+    for load in late:
+        load.wait()
     project((0, 0), 0)
     project_y((0, 0))
     project((0, 1), 0)
@@ -356,47 +384,59 @@
     project_y((0, 1))
     project_y((2, 0))
     finish_here()
-    p_local = exact(q_ref[:, 0:512], merged[:, 0:512], ((1,), (1,)))
-    finish_second()
-    p_local = p_local + exact(q_ref[:, 512:1024], merged[:, 512:1024], ((1,), (1,)))
-    pa_slots[y] = p_local.astype(BF16)
-    spread(go, "pa", lambda k: pa_slots.at[y], pa_slots, y, y_of)
+    p_first = exact(q_ref[:, 0:512], merged[:, 0:512], ((1,), (1,)))
+    for r in range(2):
+        finish_second(r)
+        rows = slice(256 * r, 256 * r + 256)
+        p_local = p_first[:, rows] + exact(q_ref[:, 512:1024], merged[rows, 512:1024], ((1,), (1,)))
+        pa_slots[r, y] = p_local.astype(BF16)
+        spread(go, ("pa", r), lambda k: pa_slots.at[r, y], pa_slots.at[r], y, y_of)
     project_y((3, 1))
+    for r in range(2):
+        gathered(go, ("pa", r), y_of)
+        pb_slots[r, zh] = total_of(pa_slots.at[r], 4).astype(BF16)
+        spread(go, ("pb", r), lambda k: pb_slots.at[r, zh], pb_slots.at[r], zh, z_of)
     project_y((1, 1))
-    gathered(go, "pa", y_of)
-    pb_slots[zh] = total_of(pa_slots, 4).astype(BF16)
-    spread(go, "pb", lambda k: pb_slots.at[zh], pb_slots, zh, z_of)
-    project_y((2, 1))
-    gathered(go, "pb", z_of)
-    factor = total_of(pb_slots, 2) * 0.125
-
-    g_slots[f] = exact(factor, factor, ((1,), (1,)))
-    spread(go, "gram", lambda k: g_slots.at[f], g_slots, f, member_of)
-    s_local = exact(factor, merged[...], ((1,), (0,))) * 0.125
+    s_local = None
+    for r in range(2):
+        gathered(go, ("pb", r), z_of)
+        rows = slice(256 * r, 256 * r + 256)
+        factor = total_of(pb_slots.at[r], 2) * 0.125
+        wide_factor[:, rows] = factor
+        s_part = exact(factor, merged[rows], ((1,), (0,)))
+        s_local = s_part if s_local is None else s_local + s_part
     for i in range(4):
         for j in range(4):
-            s_out[i * 4 + j] = s_local[16 * i : 16 * i + 16, 256 * j : 256 * j + 256]
+            s_out[i * 4 + j] = (s_local[16 * i : 16 * i + 16, 256 * j : 256 * j + 256] * 0.125).astype(BF16)
     spread(go, "s1", lambda k: s_out.at[plane_at[k]], s1, plane, plane_of)
+    mine = wide_factor[pl.ds(pl.multiple_of(d * 8, 8), 8)]
+    factor = wide_factor[...]
+    g1_slots[f] = exact(mine, factor, ((1,), (1,)))
+    spread(go, "g1", lambda k: g1_slots.at[f], g1_slots, f, member_of)
     s1[plane] = s_out[plane]
-
-    gathered(go, "gram", member_of)
-    gram = total_of(g_slots, 16)
-    row = lax.broadcasted_iota(jnp.int32, (64, 64), 0)
-    lane = lax.broadcasted_iota(jnp.int32, (64, 64), 1)
-    eye = jnp.where(row == lane, 1.0, 0.0).astype(F32)
-    work = jnp.concatenate([eye, gram], axis=1).reshape(8, 8, 128)
-    row_id = lax.broadcasted_iota(jnp.int32, (8, 8, 128), 0) * 8 + lax.broadcasted_iota(jnp.int32, (8, 8, 128), 1)
+    project_y((2, 1))
+    gathered(go, "g1", member_of)
+    g2_slots[d] = total_of(g1_slots, 16)
+    spread(go, "g2", lambda k: g2_slots.at[d], g2_slots, d, group_of)
 
     gathered(go, "s1", plane_of)
     s2[column] = total_of(s1, 16)
     spread(go, "s2", lambda k: s2.at[column], s2, column, column_of)
-    for k in range(0, 28, 4):
+    gathered(go, "g2", group_of)
+    group = lax.broadcasted_iota(jnp.int32, (8, 8, 64), 0)
+    row = lax.broadcasted_iota(jnp.int32, (8, 8, 64), 1)
+    lane = lax.broadcasted_iota(jnp.int32, (8, 8, 64), 2)
+    eye = jnp.where(group * 8 + row == lane, 1.0, 0.0).astype(F32)
+    work = jnp.concatenate([eye, g2_slots[...]], axis=2)
+    row_id = lax.broadcasted_iota(jnp.int32, (8, 8, 128), 0) * 8 + lax.broadcasted_iota(jnp.int32, (8, 8, 128), 1)
+    for k in range(0, 16, 4):
         work = eliminate(work, k, row_id)
 
     gathered(go, "s2", column_of)
-    s3[plane] = total_of(s2, 8)
-    spread(go, "s3", lambda k: s3.at[plane], s3, plane, plane_of)
-    for k in range(28, 64, 4):
+    s3_out[...] = total_of(s2, 8).astype(BF16)
+    s3[plane] = s3_out[...]
+    spread(go, "s3", lambda k: s3_out, s3, plane, plane_of)
+    for k in range(16, 64, 4):
         work = eliminate(work, k, row_id)
     lane_id = lax.broadcasted_iota(jnp.int32, (8, 8, 128), 2)
     diagonal = jnp.sum(jnp.where(lane_id == row_id + 64, work, 0.0), axis=2, keepdims=True)
@@ -409,7 +449,7 @@
     gathered(go, "s3", plane_of)
     s_total = jnp.concatenate(
         [jnp.concatenate([s3[i * 4 + j] for j in range(4)], axis=1) for i in range(4)], axis=0
-    )
+    ).astype(F32)
     q_next_ref[...] = exact(inverse, s_total, ((1,), (0,)))
     go.finish()
 
@@ -418,18 +458,18 @@
     rows, width = feedback.shape
     rank = q_t.shape[0]
     vmem = pl.BlockSpec(memory_space=pltpu.VMEM)
-    hbm = pl.BlockSpec(memory_space=pl.ANY)
+    hbm = pl.BlockSpec(memory_space=pltpu.HBM)
     dma = pltpu.SemaphoreType.DMA
     return pl.pallas_call(
         functools.partial(step_kernel, grad_scale),
         out_shape=(
-            jax.ShapeDtypeStruct(tokens.shape, BF16),
-            jax.ShapeDtypeStruct((rows, width), F32),
-            jax.ShapeDtypeStruct((rows, rank), F32),
-            jax.ShapeDtypeStruct((rank, width), F32),
+            pltpu.VMEM(tokens.shape, BF16),
+            pltpu.VMEM((rows, width), F32),
+            pltpu.VMEM((rows, rank), F32),
+            pltpu.VMEM((rank, width), F32),
         ),
-        in_specs=[hbm, hbm, hbm, vmem, vmem],
-        out_specs=(hbm, vmem, vmem, vmem),
+        in_specs=[hbm] * 5,
+        out_specs=(vmem,) * 4,
         scratch_shapes=[
             pltpu.VMEM((8, 1024, 512), BF16),
             pltpu.VMEM((1024, 1024), BF16),
@@ -440,54 +480,48 @@
             pltpu.VMEM((512, 512), BF16),
             pltpu.VMEM((4, 512, 512), BF16),
             pltpu.VMEM((8, 2, 256, 1024), BF16),
-            pltpu.VMEM((4, rank, rows), BF16),
-            pltpu.VMEM((2, rank, rows), BF16),
-            pltpu.VMEM((16, rank, rank), F32),
-            pltpu.VMEM((16, 16, 256), F32),
-            pltpu.VMEM((16, 16, 256), F32),
+            pltpu.VMEM((2, 4, rank, rows // 2), BF16),
+            pltpu.VMEM((2, 2, rank, rows // 2), BF16),
+            pltpu.VMEM((16, 8, rank), F32),
+            pltpu.VMEM((8, 8, rank), F32),
+            pltpu.VMEM((rank, rows), F32),
+            pltpu.VMEM((16, 16, 256), BF16),
+            pltpu.VMEM((16, 16, 256), BF16),
             pltpu.VMEM((8, 16, 256), F32),
-            pltpu.VMEM((16, 16, 256), F32),
-            dma((N_COPIES,)), dma((N_COPIES,)), dma((10,)), dma((16,)),
+            pltpu.VMEM((16, 256), BF16),
+            pltpu.VMEM((16, 16, 256), BF16),
+            pltpu.SemaphoreType.REGULAR((6,)),
+            pltpu.VMEM((rows, width), F32),
+            pltpu.VMEM((rank, width), F32),
+            dma((N_COPIES,)), dma((N_COPIES,)), dma((12,)), dma((16,)),
         ],
         compiler_params=pltpu.CompilerParams(
-            collective_id=2, has_side_effects=True, vmem_limit_bytes=60 * 1024 * 1024
+            collective_id=2, has_side_effects=True, vmem_limit_bytes=50 * 1024 * 1024
         ),
         name="step",
     )(tokens, cotangent, weight, feedback, q_t)
 
 
-def results_kernel(made, merged, p_hat, q_next, input_grad, feedback_next, q_out, pieces, wide, read_sem, write_sem):
-    chunk = pieces.shape[1]
-    n = pieces.shape[0]
-    first = pltpu.make_async_copy(merged, wide, read_sem.at[n])
-    first.start()
-    reads, writes = [], []
-    for i in range(n):
-        rows = pl.ds(i * chunk, chunk)
-        reads.append(pltpu.make_async_copy(made.at[rows], pieces.at[i], read_sem.at[i]))
-        writes.append(pltpu.make_async_copy(pieces.at[i], input_grad.at[rows], write_sem.at[i]))
-        reads[i].start()
-    q_out[...] = q_next[...]
-    first.wait()
-    total = wide.shape[0]
-    half = total // 2
+def results_kernel(made, merged, p_hat, q_next, input_grad, feedback_next, q_out, wide, write_sem):
+    writes = [
+        pltpu.make_async_copy(made, input_grad, write_sem.at[0]),
+        pltpu.make_async_copy(q_next, q_out, write_sem.at[1]),
+    ]
+    for write in writes:
+        write.start()
+    half = wide.shape[0] // 2
     for h in range(2):
         rows = pl.ds(h * half, half)
-        wide[rows] = wide[rows] - exact(p_hat[rows], q_next[...], ((1,), (0,)))
-        writes.append(pltpu.make_async_copy(wide.at[rows], feedback_next.at[rows], write_sem.at[n + h]))
-        writes[n + h].start()
-        for i in range(h * n // 2, (h + 1) * n // 2):
-            reads[i].wait()
-            writes[i].start()
+        wide[rows] = merged[rows] - exact(p_hat[rows], q_next[...], ((1,), (0,)))
+        writes.append(pltpu.make_async_copy(wide.at[rows], feedback_next.at[rows], write_sem.at[2 + h]))
+        writes[2 + h].start()
     for write in writes:
         write.wait()
 
 
 def results(made, merged, p_hat, q_next):
-    n = 8
     vmem = pl.BlockSpec(memory_space=pltpu.VMEM)
-    hbm = pl.BlockSpec(memory_space=pl.ANY)
-    dma = pltpu.SemaphoreType.DMA
+    hbm = pl.BlockSpec(memory_space=pltpu.HBM)
     return pl.pallas_call(
         results_kernel,
         out_shape=(
@@ -495,14 +529,10 @@
             jax.ShapeDtypeStruct(merged.shape, F32),
             jax.ShapeDtypeStruct(q_next.shape, F32),
         ),
-        in_specs=[hbm, hbm, vmem, vmem],
-        out_specs=(hbm, hbm, vmem),
-        scratch_shapes=[
-            pltpu.VMEM((n, made.shape[0] // n, made.shape[1]), BF16),
-            pltpu.VMEM(merged.shape, F32),
-            dma((n + 1,)), dma((n + 2,)),
-        ],
-        compiler_params=pltpu.CompilerParams(vmem_limit_bytes=24 * 1024 * 1024),
+        in_specs=[vmem] * 4,
+        out_specs=(hbm,) * 3,
+        scratch_shapes=[pltpu.VMEM(merged.shape, F32), pltpu.SemaphoreType.DMA((4,))],
+        compiler_params=pltpu.CompilerParams(vmem_limit_bytes=16 * 1024 * 1024),
         name="results",
     )(made, merged, p_hat, q_next)
 

time: 133 us -> 113 us (0.85)
  Pallas kernels: 125 us -> 112 us
  local copies, waits for them, and re-layouts: 6.86 us -> 0 us
    pallas_call x1, Pallas kernels: 119 us -> 108 us  [step(): pl.pallas_call(functools.partial(step_kernel, grad_scale), out_shape=(plt...]
    unnamed x8 -> x0, local copies, waits for them, and re-layouts: 6.86 us -> none
    pallas_call x1, Pallas kernels: 6.48 us -> 4.16 us  [results(): pl.pallas_call(results_kernel, out_shape=(jax.ShapeDtypeStruct(made.shape...]
where the time goes in v4:
time: 113 us
  Pallas kernels  112 us (99%)
    pallas_call x1, Pallas kernels, step(): pl.pallas_call(functools.partial(step_kernel, grad_scale), out_shape=(plt...  108 us
    pallas_call x1, Pallas kernels, results(): pl.pallas_call(results_kernel, out_shape=(jax.ShapeDtypeStruct(made.shape...  4.16 us

profile of v4, /device:TPU:0, one launch (start us, length us, event | category | flops | bytes accessed | tf_op | source)
XLA Modules:
  0.0 112.6 jit_solution(11622730454126458471)
XLA Ops:
  0.6 107.6 %step.1 = (bf16[512,8192]{1,0:T(8,128)(2,1)S(1)}, f32[512,1024]{1,0:T(8,128)S(1)}, f32[512,64]{1,0:T(8,128)S(1)}, f32[64,1024]{1,0:T(8,128)S(1)}) custom-call(bf16[512,8192]{1,0:T(8,128)(2,1)} %tokens.1, bf16[512,1024]{1,0:T(8,128)(2,1)} %cotangent.1, bf16[512,1024]{1,0:T(8,128)(2,1)} %weight.1, f32[512,1024]{1,0:T(8,128)} %bitcast.4, f32[64,1024]{1,0:T(8,128)} %bitcast.5), custom_call_target="tpu_custom_call" | custom-call | tf_op jit(solution)/shard_map/step/pallas_call | solution.py:463
  108.3 4.2 %results.1 = (bf16[512,8192]{1,0:T(8,128)(2,1)}, f32[512,1024]{1,0:T(8,128)}, f32[64,1024]{1,0:T(8,128)}) custom-call(bf16[512,8192]{1,0:T(8,128)(2,1)S(1)} %get-tuple-element.10.made, f32[512,1024]{1,0:T(8,128)S(1)} %get-tuple-element.11.merged, f32[512,64]{1,0:T(8,128)S(1)} %get-tuple-element.12.p_hat, f32[64,1024]{1,0:T(8,128)S(1)} %get-tuple-element.13.q_next), custom_call_target="tpu_custom_call" | custom-call | tf_op jit(solution)/shard_map/results/pallas_call | solution.py:525

commit v5 on v4

--- a/solution.py
+++ b/solution.py
@@ -68,7 +68,6 @@
 
 ORDER = [(2, 1), (1, 1), (3, 1), (0, 1), (2, 0), (1, 0), (3, 0), (0, 0)]
 SLOT = {relative: o for o, relative in enumerate(ORDER)}
-Y_UP = [(0, 0), (3, 0), (2, 0), (1, 1)]
 N_COPIES = 160
 
 
@@ -104,7 +103,6 @@
     feedback, q_ref, send, recv, load_sem, store_sem,
 ):
     zh, y, x, zl, c = where_am_i()
-    half = y % 2
     mate = device(zh, y, x, zl, 1 - c)
     x_up, x_down = device(zh, y, (x + 1) % 4, zl, c), device(zh, y, (x + 3) % 4, zl, c)
     y_up, y_down = device(zh, (y + 1) % 4, x, zl, c), device(zh, (y + 3) % 4, x, zl, c)
@@ -152,37 +150,51 @@
                 pl.semaphore_signal(met.at[n], inc=1, device_id=target, device_id_type=MESH)
 
     go = Copies(send, recv)
-    go.start("cot", cotangent, cot.at[512:1024], mate)
+    go.start(("cot", 1), cotangent.at[:, 512:1024], cot.at[512:1024, 512:1024], mate)
     for o, relative in enumerate(ORDER):
         columns = pl.ds(pl.multiple_of(first_row(relative, 1 - c), 512), 512)
         go.start(("tok", o), tokens.at[:, columns], tok.at[o, 512:1024], mate)
-
-    my_half = weight.at[pl.ds(pl.multiple_of(half * 256, 256), 256)]
-    own_half = pltpu.make_async_copy(my_half, w_all.at[SLOT[0, 0], 0], load_sem.at[9])
-    own_half.start()
-    go.start(("wx", 3), my_half, w_all.at[SLOT[3, 0], 0], x_up)
-    go.start(("wx", 1), my_half, w_all.at[SLOT[1, 0], 0], x_down)
-    go.start(("wz", 0), my_half, w_all.at[SLOT[0, 1], 0], z_across)
-    go.start(("wy", (0, 0)), my_half, w_all.at[SLOT[0, 0], 1], y_up)
+        if o == 0:
+            go.start(("cot", 0), cotangent.at[:, 0:512], cot.at[512:1024, 0:512], mate)
+
+    def quarter(of, start=0, size=128):
+        return pl.ds(pl.multiple_of(of * 128 + start, 64), size)
+
+    mine = quarter(y)
+    below, above = (y + 3) % 4, (y + 1) % 4
+    own_shard = pltpu.make_async_copy(weight, w_all.at[SLOT[0, 0]], load_sem.at[9])
+    own_shard.start()
+    go.start(("wx", 3), weight.at[mine], w_all.at[SLOT[3, 0], mine], x_up)
+    go.start(("wx", 1), weight.at[mine], w_all.at[SLOT[1, 0], mine], x_down)
+    go.start(("w0", 0), weight.at[0:256], w_all.at[SLOT[0, 1], 0:256], z_across)
+
+    def same(name, relative, rows, target):
+        src = w_all.at[SLOT[relative], rows]
+        go.start((name, relative), src, src, target)
 
     def weight_y(relative):
-        target = y_up if relative in Y_UP else y_down
-        go.start(("wy", relative), w_all.at[SLOT[relative], 0], w_all.at[SLOT[relative], 1], target)
+        same("yu", relative, mine, y_up)
+        same("yd", relative, mine, y_down)
+
+    def forward_y(relative):
+        go.arrived(("yu", relative))
+        same("fu", relative, quarter(below, 0, 64), y_up)
+        go.arrived(("yd", relative))
+        same("fd", relative, quarter(above, 64, 64), y_down)
 
     def weight_x():
-        go.arrived(("wx", 3))
-        go.start(("wf", 0), w_all.at[SLOT[3, 0], 0, 0:128], w_all.at[SLOT[2, 0], 0, 0:128], x_up)
-        go.start(("wz", 3), w_all.at[SLOT[3, 0], 0], w_all.at[SLOT[3, 1], 0], z_across)
-        weight_y((3, 0))
-        go.arrived(("wx", 1))
-        go.start(("wf", 1), w_all.at[SLOT[1, 0], 0, 128:256], w_all.at[SLOT[2, 0], 0, 128:256], x_down)
-        go.start(("wz", 1), w_all.at[SLOT[1, 0], 0], w_all.at[SLOT[1, 1], 0], z_across)
-        weight_y((1, 0))
+        for rx, start, target in ((3, 0, x_up), (1, 64, x_down)):
+            go.arrived(("wx", rx))
+            rows = quarter(y, start, 64)
+            go.start(("wf", rx), w_all.at[SLOT[rx, 0], rows], w_all.at[SLOT[2, 0], rows], target)
+            go.start(("wz", rx), w_all.at[SLOT[rx, 0], mine], w_all.at[SLOT[rx, 1], mine], z_across)
+            weight_y((rx, 0))
 
     def weight_opposite():
-        go.arrived(("wf", 0))
+        go.arrived(("wf", 3))
         go.arrived(("wf", 1))
-        go.start(("wz", 2), w_all.at[SLOT[2, 0], 0], w_all.at[SLOT[2, 1], 0], z_across)
+        go.start(("wz", 2), w_all.at[SLOT[2, 0], mine], w_all.at[SLOT[2, 1], mine], z_across)
+        go.start(("w0", 1), weight.at[256:512], w_all.at[SLOT[0, 1], 256:512], z_across)
         weight_y((2, 0))
 
     def weight_z(rx):
@@ -191,28 +203,46 @@
 
     stores = []
 
-    def project(relative, which):
+    def project(relative):
         n = len(stores)
         slot = SLOT[relative]
+        if relative == (0, 0):
+            own_shard.wait()
+        elif relative == (0, 1):
+            go.arrived(("w0", 0))
+            go.arrived(("w0", 1))
+        else:
+            go.arrived(("fu", relative))
+            go.arrived(("fd", relative))
 
         @pl.loop(0, 4)
         def _(i):
             rows = pl.ds(pl.multiple_of(i * 256, 256), 256)
-            tok[slot, rows, 256 * which : 256 * which + 256] = lax.dot_general(
-                cot[rows], w_all[slot, which], (((1,), (1,)), ((), ())), preferred_element_type=F32
+            tok[slot, rows] = lax.dot_general(
+                cot[rows], w_all[slot], (((1,), (1,)), ((), ())), preferred_element_type=F32
             ).astype(BF16)
 
-        column = first_row(relative, c) + (half if which == 0 else 1 - half) * 256
-        columns = pl.ds(pl.multiple_of(column, 256), 256)
-        made = tok.at[slot, :, 256 * which : 256 * which + 256]
+        columns = pl.ds(pl.multiple_of(first_row(relative, c), 512), 512)
+        made = tok.at[slot]
         store = pltpu.make_async_copy(made.at[0:512], input_grad.at[:, columns], store_sem.at[n])
         store.start()
         stores.append(store)
         go.start(("out", n), made.at[512:1024], input_grad.at[:, columns], mate)
 
-    def project_y(relative):
-        go.arrived(("wy", relative))
-        project(relative, 1)
+    def first_partial(color):
+        if color == 1:
+            loads[0].wait()
+            loads[1].wait()
+            go.arrived(("tok", 0))
+        go.arrived(("cot", color))
+        columns = slice(512 * color, 512 * color + 512)
+
+        @pl.loop(0, 2)
+        def _(i):
+            rows = pl.ds(pl.multiple_of(i * 256, 256), 256)
+            part[0, rows, columns] = lax.dot_general(
+                tok[0, :, rows], cot[:, columns], (((0,), (0,)), ((), ())), preferred_element_type=F32
+            ).astype(BF16)
 
     def partial(o):
         loads[1 + o].wait()
@@ -288,13 +318,16 @@
                 + side[0, 1, rows].astype(F32)
             ).astype(BF16)
 
-        go.start("z2", z_send, z_last, z_pair)
-
-    def finish_here():
-        sides_arrived(1)
-        go.arrived("z2")
-
-        @pl.loop(0, 4)
+        for r in range(2):
+            rows = pl.ds(256 * r, 256)
+            go.start(("z2", r), z_send.at[rows], z_last.at[rows], z_pair)
+
+    def finish_here(r):
+        if r == 0:
+            sides_arrived(1)
+        go.arrived(("z2", r))
+
+        @pl.loop(2 * r, 2 * r + 2)
         def _(i):
             rows = pl.ds(pl.multiple_of(i * 128, 128), 128)
             total = (
@@ -324,16 +357,16 @@
             )
             merged[rows, 512:1024] = feedback[rows, 512:1024] + total * grad_scale
 
-    loads[0].wait()
-    go.arrived("cot")
-    partial(0)
+    first_partial(1)
+    z_exchange(2)
+    first_partial(0)
+    opposite(0)
     meet(0)
-    opposite(0)
-    z_exchange(2)
     partial(1)
     meet(1)
     beside_up(0)
     z_exchange(1)
+    weight_x()
     partial(2)
     meet(2)
     beside_down(0)
@@ -341,86 +374,81 @@
     partial(3)
     meet(3)
     z_exchange(0)
-    weight_x()
     partial(4)
     meet(4)
     opposite(1)
-    weight_z(0)
     partial(5)
     meet(5)
     beside_up(1)
     pass_on(0)
+    forward_y((3, 0))
     partial(6)
     meet(6)
     beside_down(1)
     z_sum(2)
     opposite(2)
+    weight_opposite()
     partial(7)
-    own_half.wait()
+    forward_y((1, 0))
+    weight_z(3)
+    weight_z(1)
     for load in late:
         load.wait()
-    project((0, 0), 0)
-    project_y((0, 0))
-    project((0, 1), 0)
-    weight_z(3)
-    project((3, 0), 0)
-    project((1, 0), 0)
-    weight_opposite()
+    project((0, 0))
     z_sum(1)
     beside_up(2)
-    project((3, 1), 0)
-    project((2, 0), 0)
+    weight_z(2)
     pass_on(1)
-    weight_z(1)
-    project((1, 1), 0)
+    project((3, 0))
+    forward_y((2, 0))
+    project((1, 0))
     finish_across()
     z_sum(3)
     beside_down(2)
-    project_y((3, 0))
-    project_y((1, 0))
-    weight_z(2)
-    project((2, 1), 0)
+    forward_y((3, 1))
+    project((0, 1))
+    forward_y((1, 1))
     pass_on(2)
-    project_y((0, 1))
-    project_y((2, 0))
-    finish_here()
-    p_first = exact(q_ref[:, 0:512], merged[:, 0:512], ((1,), (1,)))
+    forward_y((2, 1))
+    project((2, 0))
+    project((3, 1))
     for r in range(2):
+        finish_here(r)
         finish_second(r)
         rows = slice(256 * r, 256 * r + 256)
-        p_local = p_first[:, rows] + exact(q_ref[:, 512:1024], merged[rows, 512:1024], ((1,), (1,)))
+        p_local = exact(q_ref[...], merged[rows], ((1,), (1,)))
         pa_slots[r, y] = p_local.astype(BF16)
         spread(go, ("pa", r), lambda k: pa_slots.at[r, y], pa_slots.at[r], y, y_of)
-    project_y((3, 1))
+    project((1, 1))
     for r in range(2):
         gathered(go, ("pa", r), y_of)
         pb_slots[r, zh] = total_of(pa_slots.at[r], 4).astype(BF16)
         spread(go, ("pb", r), lambda k: pb_slots.at[r, zh], pb_slots.at[r], zh, z_of)
-    project_y((1, 1))
     s_local = None
     for r in range(2):
         gathered(go, ("pb", r), z_of)
         rows = slice(256 * r, 256 * r + 256)
         factor = total_of(pb_slots.at[r], 2) * 0.125
         wide_factor[:, rows] = factor
+        if r == 1:
+            slice_of_p = wide_factor[pl.ds(pl.multiple_of(d * 8, 8), 8)]
+            g1_slots[f] = exact(slice_of_p, wide_factor[...], ((1,), (1,)))
+            spread(go, "g1", lambda k: g1_slots.at[f], g1_slots, f, member_of)
         s_part = exact(factor, merged[rows], ((1,), (0,)))
         s_local = s_part if s_local is None else s_local + s_part
+    factor = wide_factor[...]
     for i in range(4):
         for j in range(4):
             s_out[i * 4 + j] = (s_local[16 * i : 16 * i + 16, 256 * j : 256 * j + 256] * 0.125).astype(BF16)
     spread(go, "s1", lambda k: s_out.at[plane_at[k]], s1, plane, plane_of)
-    mine = wide_factor[pl.ds(pl.multiple_of(d * 8, 8), 8)]
-    factor = wide_factor[...]
-    g1_slots[f] = exact(mine, factor, ((1,), (1,)))
-    spread(go, "g1", lambda k: g1_slots.at[f], g1_slots, f, member_of)
     s1[plane] = s_out[plane]
-    project_y((2, 1))
+    project((2, 1))
     gathered(go, "g1", member_of)
     g2_slots[d] = total_of(g1_slots, 16)
     spread(go, "g2", lambda k: g2_slots.at[d], g2_slots, d, group_of)
 
     gathered(go, "s1", plane_of)
-    s2[column] = total_of(s1, 16)
+    s2[column] = total_of(s1, 16).astype(BF16)
     spread(go, "s2", lambda k: s2.at[column], s2, column, column_of)
     gathered(go, "g2", group_of)
     group = lax.broadcasted_iota(jnp.int32, (8, 8, 64), 0)
@@ -443,7 +471,7 @@
     inverse = (work * (1.0 / jnp.sqrt(diagonal))).reshape(64, 128)[:, :64]
     p_hat_ref[...] = jnp.transpose(exact(inverse, factor, ((1,), (0,))))
 
-    for n in range(16):
+    for n in range(8):
         go.arrived(("out", n))
         stores[n].wait()
     gathered(go, "s3", plane_of)
@@ -479,7 +507,7 @@
             pltpu.VMEM((512, 512), BF16),
             pltpu.VMEM((512, 512), BF16),
             pltpu.VMEM((4, 512, 512), BF16),
-            pltpu.VMEM((8, 2, 256, 1024), BF16),
+            pltpu.VMEM((8, 512, 1024), BF16),
             pltpu.VMEM((2, 4, rank, rows // 2), BF16),
             pltpu.VMEM((2, 2, rank, rows // 2), BF16),
             pltpu.VMEM((16, 8, rank), F32),
@@ -487,7 +515,7 @@
             pltpu.VMEM((rank, rows), F32),
             pltpu.VMEM((16, 16, 256), BF16),
             pltpu.VMEM((16, 16, 256), BF16),
-            pltpu.VMEM((8, 16, 256), F32),
+            pltpu.VMEM((8, 16, 256), BF16),
             pltpu.VMEM((16, 256), BF16),
             pltpu.VMEM((16, 16, 256), BF16),
             pltpu.SemaphoreType.REGULAR((6,)),

time: 113 us -> 105 us (0.929)
  Pallas kernels: 112 us -> 104 us
    pallas_call x1, Pallas kernels: 108 us -> 99.7 us  [step(): pl.pallas_call(functools.partial(step_kernel, grad_scale), out_shape=(plt...]
where the time goes in v5:
time: 105 us
  Pallas kernels  104 us (99%)
    pallas_call x1, Pallas kernels, step(): pl.pallas_call(functools.partial(step_kernel, grad_scale), out_shape=(plt...  99.7 us
    pallas_call x1, Pallas kernels, results(): pl.pallas_call(results_kernel, out_shape=(jax.ShapeDtypeStruct(made.shape...  4.16 us

profile of v5, /device:TPU:0, one launch (start us, length us, event | category | flops | bytes accessed | tf_op | source)
XLA Modules:
  0.0 104.7 jit_solution(11460316412665555605)
XLA Ops:
  0.6 99.7 %step.1 = (bf16[512,8192]{1,0:T(8,128)(2,1)S(1)}, f32[512,1024]{1,0:T(8,128)S(1)}, f32[512,64]{1,0:T(8,128)S(1)}, f32[64,1024]{1,0:T(8,128)S(1)}) custom-call(bf16[512,8192]{1,0:T(8,128)(2,1)} %tokens.1, bf16[512,1024]{1,0:T(8,128)(2,1)} %cotangent.1, bf16[512,1024]{1,0:T(8,128)(2,1)} %weight.1, f32[512,1024]{1,0:T(8,128)} %bitcast.4, f32[64,1024]{1,0:T(8,128)} %bitcast.5), custom_call_target="tpu_custom_call" | custom-call | tf_op jit(solution)/shard_map/step/pallas_call | solution.py:491
  100.4 4.2 %results.1 = (bf16[512,8192]{1,0:T(8,128)(2,1)}, f32[512,1024]{1,0:T(8,128)}, f32[64,1024]{1,0:T(8,128)}) custom-call(bf16[512,8192]{1,0:T(8,128)(2,1)S(1)} %get-tuple-element.10.made, f32[512,1024]{1,0:T(8,128)S(1)} %get-tuple-element.11.merged, f32[512,64]{1,0:T(8,128)S(1)} %get-tuple-element.12.p_hat, f32[64,1024]{1,0:T(8,128)S(1)} %get-tuple-element.13.q_next), custom_call_target="tpu_custom_call" | custom-call | tf_op jit(solution)/shard_map/results/pallas_call | solution.py:553

commit v6 on v5

--- a/solution.py
+++ b/solution.py
@@ -47,12 +47,13 @@
 
 def eliminate(work, k, row_id):
     group, first = k // 8, k % 8
-    columns = [jnp.broadcast_to(work[:, :, 64 + k + j : 65 + k + j], (8, 8, 128)) for j in range(4)]
-    rows = [jnp.broadcast_to(work[group, first + j : first + j + 1, :], (8, 128)) for j in range(4)]
+    done, work, row_id = work[:group], work[group:], row_id[group:]
+    columns = [jnp.broadcast_to(work[:, :, 64 + k + j : 65 + k + j], work.shape) for j in range(4)]
+    rows = [jnp.broadcast_to(work[0, first + j : first + j + 1, :], (8, 128)) for j in range(4)]
     pivot = {}
     for j in range(4):
         for i in range(j, 4):
-            pivot[i, j] = jnp.broadcast_to(columns[j][group, first + i : first + i + 1, :], (8, 128))
+            pivot[i, j] = jnp.broadcast_to(columns[j][0, first + i : first + i + 1, :], (8, 128))
     for j in range(4):
         inverse = 1.0 / pivot[j, j]
         multiplier = columns[j] * inverse
@@ -63,12 +64,14 @@
             for m in range(i, 4):
                 pivot[m, i] = pivot[m, i] - scale * pivot[m, j]
         work = work - jnp.where(row_id > k + j, multiplier, 0.0) * rows[j]
-    return work
+    return work if group == 0 else jnp.concatenate([done, work], axis=0)
 
 
 ORDER = [(2, 1), (1, 1), (3, 1), (0, 1), (2, 0), (1, 0), (3, 0), (0, 0)]
 SLOT = {relative: o for o, relative in enumerate(ORDER)}
-N_COPIES = 160
+N_COPIES = 176
+PARTS = 4
+ROWS = 512 // PARTS
 
 
 class Copies:
@@ -287,8 +290,8 @@
             go.arrived(("hop", s, which))
             mine = part.at[SLOT[rx, ACROSS[s]]]
             add_into(mine, columns_of(s, which), hop.at[s, which], pl.ds(0, 256))
-            for r in range(2 if s == 2 else 1):
-                rows = pl.ds(256 * r, 256) if s == 2 else pl.ds(0, 512)
+            for r in range(PARTS if s == 2 else 1):
+                rows = pl.ds(ROWS * r, ROWS) if s == 2 else pl.ds(0, 512)
                 go.start(
                     ("side", s, which, which) if s < 2 else ("last", which, r), mine.at[rows, columns_of(s, which)],
                     side.at[s, which, rows, 256 * which : 256 * which + 256], target,
@@ -318,8 +321,8 @@
                 + side[0, 1, rows].astype(F32)
             ).astype(BF16)
 
-        for r in range(2):
-            rows = pl.ds(256 * r, 256)
+        for r in range(PARTS):
+            rows = pl.ds(ROWS * r, ROWS)
             go.start(("z2", r), z_send.at[rows], z_last.at[rows], z_pair)
 
     def finish_here(r):
@@ -327,7 +330,7 @@
             sides_arrived(1)
         go.arrived(("z2", r))
 
-        @pl.loop(2 * r, 2 * r + 2)
+        @pl.loop(r * 4 // PARTS, (r + 1) * 4 // PARTS)
         def _(i):
             rows = pl.ds(pl.multiple_of(i * 128, 128), 128)
             total = (
@@ -346,7 +349,7 @@
         for which in range(2):
             go.arrived(("last", which, r))
 
-        @pl.loop(2 * r, 2 * r + 2)
+        @pl.loop(r * 4 // PARTS, (r + 1) * 4 // PARTS)
         def _(i):
             rows = pl.ds(pl.multiple_of(i * 128, 128), 128)
             total = (
@@ -412,30 +415,30 @@
     forward_y((2, 1))
     project((2, 0))
     project((3, 1))
-    for r in range(2):
+    for r in range(PARTS):
         finish_here(r)
         finish_second(r)
-        rows = slice(256 * r, 256 * r + 256)
+        rows = slice(ROWS * r, ROWS * r + ROWS)
         p_local = exact(q_ref[...], merged[rows], ((1,), (1,)))
         pa_slots[r, y] = p_local.astype(BF16)
         spread(go, ("pa", r), lambda k: pa_slots.at[r, y], pa_slots.at[r], y, y_of)
     project((1, 1))
-    for r in range(2):
+    for r in range(PARTS):
         gathered(go, ("pa", r), y_of)
         pb_slots[r, zh] = total_of(pa_slots.at[r], 4).astype(BF16)
         spread(go, ("pb", r), lambda k: pb_slots.at[r, zh], pb_slots.at[r], zh, z_of)
     s_local = None
-    for r in range(2):
+    for r in range(PARTS):
         gathered(go, ("pb", r), z_of)
-        rows = slice(256 * r, 256 * r + 256)
-        factor = total_of(pb_slots.at[r], 2) * 0.125
-        wide_factor[:, rows] = factor
-        if r == 1:
+        wide_factor[:, ROWS * r : ROWS * r + ROWS] = total_of(pb_slots.at[r], 2) * 0.125
+        if r == PARTS - 1:
             slice_of_p = wide_factor[pl.ds(pl.multiple_of(d * 8, 8), 8)]
             g1_slots[f] = exact(slice_of_p, wide_factor[...], ((1,), (1,)))
             spread(go, "g1", lambda k: g1_slots.at[f], g1_slots, f, member_of)
-        s_part = exact(factor, merged[rows], ((1,), (0,)))
-        s_local = s_part if s_local is None else s_local + s_part
+        if (r + 1) * ROWS % 256 == 0:
+            rows = slice((r + 1) * ROWS - 256, (r + 1) * ROWS)
+            s_part = exact(wide_factor[:, rows], merged[rows], ((1,), (0,)))
+            s_local = s_part if s_local is None else s_local + s_part
     factor = wide_factor[...]
     for i in range(4):
         for j in range(4):
@@ -457,14 +460,14 @@
     eye = jnp.where(group * 8 + row == lane, 1.0, 0.0).astype(F32)
     work = jnp.concatenate([eye, g2_slots[...]], axis=2)
     row_id = lax.broadcasted_iota(jnp.int32, (8, 8, 128), 0) * 8 + lax.broadcasted_iota(jnp.int32, (8, 8, 128), 1)
-    for k in range(0, 16, 4):
+    for k in range(0, 24, 4):
         work = eliminate(work, k, row_id)
 
     gathered(go, "s2", column_of)
     s3_out[...] = total_of(s2, 8).astype(BF16)
     s3[plane] = s3_out[...]
     spread(go, "s3", lambda k: s3_out, s3, plane, plane_of)
-    for k in range(16, 64, 4):
+    for k in range(24, 64, 4):
         work = eliminate(work, k, row_id)
     lane_id = lax.broadcasted_iota(jnp.int32, (8, 8, 128), 2)
     diagonal = jnp.sum(jnp.where(lane_id == row_id + 64, work, 0.0), axis=2, keepdims=True)
@@ -508,8 +511,8 @@
             pltpu.VMEM((512, 512), BF16),
             pltpu.VMEM((4, 512, 512), BF16),
             pltpu.VMEM((8, 512, 1024), BF16),
-            pltpu.VMEM((2, 4, rank, rows // 2), BF16),
-            pltpu.VMEM((2, 2, rank, rows // 2), BF16),
+            pltpu.VMEM((PARTS, 4, rank, ROWS), BF16),
+            pltpu.VMEM((PARTS, 2, rank, ROWS), BF16),
             pltpu.VMEM((16, 8, rank), F32),
             pltpu.VMEM((8, 8, rank), F32),
             pltpu.VMEM((rank, rows), F32),

time: 105 us -> 103 us (0.981)
  Pallas kernels: 104 us -> 102 us
    pallas_call x1, Pallas kernels: 99.7 us -> 98.2 us  [step(): pl.pallas_call(functools.partial(step_kernel, grad_scale), out_shape=(plt...]
where the time goes in v6:
time: 103 us
  Pallas kernels  102 us (99%)
    pallas_call x1, Pallas kernels, step(): pl.pallas_call(functools.partial(step_kernel, grad_scale), out_shape=(plt...  98.2 us
    pallas_call x1, Pallas kernels, results(): pl.pallas_call(results_kernel, out_shape=(jax.ShapeDtypeStruct(made.shape...  4.16 us

profile of v6, /device:TPU:0, one launch (start us, length us, event | category | flops | bytes accessed | tf_op | source)
XLA Modules:
  0.0 103.1 jit_solution(12347439694763025233)
XLA Ops:
  0.6 98.2 %step.1 = (bf16[512,8192]{1,0:T(8,128)(2,1)S(1)}, f32[512,1024]{1,0:T(8,128)S(1)}, f32[512,64]{1,0:T(8,128)S(1)}, f32[64,1024]{1,0:T(8,128)S(1)}) custom-call(bf16[512,8192]{1,0:T(8,128)(2,1)} %tokens.1, bf16[512,1024]{1,0:T(8,128)(2,1)} %cotangent.1, bf16[512,1024]{1,0:T(8,128)(2,1)} %weight.1, f32[512,1024]{1,0:T(8,128)} %bitcast.4, f32[64,1024]{1,0:T(8,128)} %bitcast.5), custom_call_target="tpu_custom_call" | custom-call | tf_op jit(solution)/shard_map/step/pallas_call | solution.py:494
  98.8 4.2 %results.1 = (bf16[512,8192]{1,0:T(8,128)(2,1)}, f32[512,1024]{1,0:T(8,128)}, f32[64,1024]{1,0:T(8,128)}) custom-call(bf16[512,8192]{1,0:T(8,128)(2,1)S(1)} %get-tuple-element.10.made, f32[512,1024]{1,0:T(8,128)S(1)} %get-tuple-element.11.merged, f32[512,64]{1,0:T(8,128)S(1)} %get-tuple-element.12.p_hat, f32[64,1024]{1,0:T(8,128)S(1)} %get-tuple-element.13.q_next), custom_call_target="tpu_custom_call" | custom-call | tf_op jit(solution)/shard_map/results/pallas_call | solution.py:556

commit v7 on v6

--- a/solution.py
+++ b/solution.py
@@ -74,6 +74,13 @@
 ROWS = 512 // PARTS
 
 
+def far_first(n, m, weights):
+    def length(step):
+        return weights[0] * min(step[0], n - step[0]) + weights[1] * min(step[1], m - step[1])
+
+    return sorted([(i, k) for i in range(n) for k in range(m) if i + k > 0], key=length, reverse=True)
+
+
 class Copies:
     def __init__(self, send, recv):
         self.send, self.recv, self.used, self.all = send, recv, 0, {}
@@ -114,14 +121,19 @@
     f = lax.axis_index("fsdp")
     plane = x * 4 + y
     column = zh * 4 + zl * 2 + c
-    y_of = [device(zh, (y + k) % 4, x, zl, c) for k in range(1, 4)]
+    z = zh * 2 + zl
+    y_of = [device(zh, (y + k) % 4, x, zl, c) for k in (2, 1, 3)]
     z_of = [device(1 - zh, y, x, zl, c)]
-    group_of = [((d + k) % 8, f) for k in range(1, 8)]
-    member_of = [(d, (f + k) % 16) for k in range(1, 16)]
-    plane_at = [(plane + k) % 16 for k in range(1, 16)]
-    plane_of = [device(zh, t % 4, t // 4, zl, c) for t in plane_at]
-    column_at = [(column + k) % 8 for k in range(1, 8)]
-    column_of = [device(t // 4, y, x, (t // 2) % 2, t % 2) for t in column_at]
+    group_of = [device((zh + i) % 2, (y + k) % 4, x, zl, c) for i, k in far_first(2, 4, (2, 1))]
+    member_of = [
+        device(zh, y, (x + i) % 4, (zl + k // 2) % 2, (c + k) % 2) for i, k in far_first(4, 4, (1, 0.4))
+    ]
+    plane_step = far_first(4, 4, (1, 1))
+    plane_at = [((x + i) % 4) * 4 + (y + k) % 4 for i, k in plane_step]
+    plane_of = [device(zh, (y + k) % 4, (x + i) % 4, zl, c) for i, k in plane_step]
+    column_of = [
+        device(((z + i) % 4) // 2, y, x, ((z + i) % 4) % 2, (c + k) % 2) for i, k in far_first(4, 2, (1, 0.1))
+    ]
     partners = [mate, x_up, x_down, y_up, y_down, z_pair, z_across]
 
     def first_row(relative, core):

time: 103 us -> 102 us (level)
    pallas_call x1, Pallas kernels: 98.2 us -> 97.1 us  [step(): pl.pallas_call(functools.partial(step_kernel, grad_scale), out_shape=(plt...]
where the time goes in v7:
time: 102 us
  Pallas kernels  101 us (99%)
    pallas_call x1, Pallas kernels, step(): pl.pallas_call(functools.partial(step_kernel, grad_scale), out_shape=(plt...  97.1 us
    pallas_call x1, Pallas kernels, results(): pl.pallas_call(results_kernel, out_shape=(jax.ShapeDtypeStruct(made.shape...  4.16 us

profile of v7, /device:TPU:0, one launch (start us, length us, event | category | flops | bytes accessed | tf_op | source)
XLA Modules:
  0.0 102.0 jit_solution(810490096311349291)
XLA Ops:
  0.6 97.1 %step.1 = (bf16[512,8192]{1,0:T(8,128)(2,1)S(1)}, f32[512,1024]{1,0:T(8,128)S(1)}, f32[512,64]{1,0:T(8,128)S(1)}, f32[64,1024]{1,0:T(8,128)S(1)}) custom-call(bf16[512,8192]{1,0:T(8,128)(2,1)} %tokens.1, bf16[512,1024]{1,0:T(8,128)(2,1)} %cotangent.1, bf16[512,1024]{1,0:T(8,128)(2,1)} %weight.1, f32[512,1024]{1,0:T(8,128)} %bitcast.4, f32[64,1024]{1,0:T(8,128)} %bitcast.5), custom_call_target="tpu_custom_call" | custom-call | tf_op jit(solution)/shard_map/step/pallas_call | solution.py:506
  97.7 4.2 %results.1 = (bf16[512,8192]{1,0:T(8,128)(2,1)}, f32[512,1024]{1,0:T(8,128)}, f32[64,1024]{1,0:T(8,128)}) custom-call(bf16[512,8192]{1,0:T(8,128)(2,1)S(1)} %get-tuple-element.10.made, f32[512,1024]{1,0:T(8,128)S(1)} %get-tuple-element.11.merged, f32[512,64]{1,0:T(8,128)S(1)} %get-tuple-element.12.p_hat, f32[64,1024]{1,0:T(8,128)S(1)} %get-tuple-element.13.q_next), custom_call_target="tpu_custom_call" | custom-call | tf_op jit(solution)/shard_map/results/pallas_call | solution.py:568
